TPU v7x, 32 devices: a whole 2x2x4 slice. The times are simulated.
32 devices in a mesh: groups: 2 (over x), ctx: 16 (over z, y, core).
Axes of the slice: x: 2, y: 2, z: 4, core: 2. Of those that a mesh axis runs over, the one named last changes fastest.
Arguments:
- queries: bfloat16 [2560, 4096], P(('groups', 'ctx')), parts along dimension 0, may hold values from -200 to 200
- fresh_key_value: bfloat16 [2, 2560, 512], P(None, ('groups', 'ctx')), parts along dimension 1, may hold values from -6 to 6
- cache_key_value: bfloat16 [2, 4096, 512], P(None, ('groups', 'ctx')), parts along dimension 1, may hold values from -6 to 6
- residual: bfloat16 [2560, 2048], P(('groups', 'ctx')), parts along dimension 0, may hold values from -6 to 6
- norm_gain: float32 [2048], replicated, may hold values from 0.5 to 2
- out_proj: bfloat16 [4096, 2048], P('ctx'), may hold values from -0.09375 to 0.09375
- w_gate_up: bfloat16 [32, 2048, 1536], P('ctx'), may hold values from -0.125 to 0.125
- w_down: bfloat16 [32, 768, 2048], P('ctx'), may hold values from -0.21875 to 0.21875
- route_ids: int32 [2560, 8], P(('groups', 'ctx')), parts along dimension 0, may hold values from 0 to 31, all different within a row; in each aligned block of 80 rows (0 to 79, 80 to 159, ...) at most 30 rows name the same one
- route_weights: float32 [2560, 8], P(('groups', 'ctx')), parts along dimension 0, may hold values from 0.05 to 1
- placement: int32 [32], replicated, may hold values from 0 to 31, each once
Outputs:
- hidden: bfloat16 [2560, 2048], P(('groups', 'ctx')), parts along dimension 0
- expert_out: bfloat16 [2560, 2048], P(('groups', 'ctx')), parts along dimension 0
There are 2 independent parts, one for each index of `groups`. A program takes and returns all parts, laid end to end along the dimension named above; an argument that names none is the same for every part. Nothing has to cross between parts.
Inputs may be any that keep to these rules, and one draw needn't show every extreme that they name: `route_ids`: among the rows of one index of ctx, no expert is named by more than 30 rows, a bound that some block reaches. `placement`: every slot once; slot s is the first index of w_gate_up and w_down.
All inputs are finite; a program needn't handle non-finite values.
Results may differ from a plain program's by a relative error of at most 0.017.
Values may be sent and summed in bfloat16 or wider, within the bound.
A program may use at most 128 MiB of HBM per device.

v0:
```python
import jax
import jax.numpy as jnp
from jax import lax
from jax.sharding import PartitionSpec as P

D = 2048
QUERY_HEADS = 32
KEY_VALUE_HEADS = 4
HEAD_SIZE = 128
FF = 768
TOPK = 8


epsilon = 1e-06


def local(
    queries,
    fresh_key_value,
    cache_key_value,
    residual,
    norm_gain,
    out_proj,
    w_gate_up,
    w_down,
    route_ids,
    route_weights,
    placement,
):
    count_of_rows = queries.shape[0]
    query_group_width = QUERY_HEADS // KEY_VALUE_HEADS
    scale_for_scores = HEAD_SIZE ** (-0.5)
    heads_of_query = queries.reshape(count_of_rows, KEY_VALUE_HEADS, query_group_width, HEAD_SIZE)
    self_keys = fresh_key_value[0].reshape(count_of_rows, KEY_VALUE_HEADS, HEAD_SIZE)
    self_values = fresh_key_value[1].reshape(count_of_rows, KEY_VALUE_HEADS, HEAD_SIZE)
    self_score = (
        jnp.einsum("ejaz,ejz->eja", heads_of_query, self_keys, preferred_element_type=jnp.float32)
        * scale_for_scores
    )
    start_carry = (
        self_score,
        jnp.ones_like(self_score),
        jnp.broadcast_to(self_values.astype(jnp.float32)[:, :, None, :], heads_of_query.shape),
    )

    def absorb_block(carried, block_pair):
        running_max, totals, weighted_total = carried
        block_keys, block_values = block_pair
        scores = (
            jnp.einsum(
                "rkgd,jkd->rkgj", heads_of_query, block_keys, preferred_element_type=jnp.float32
            )
            * scale_for_scores
        )
        new_max = jnp.maximum(running_max, jnp.max(scores, axis=-1))
        reduce_factor = jnp.exp(running_max - new_max)
        weights = jnp.exp(scores - new_max[..., None])
        totals = totals * reduce_factor + jnp.sum(weights, axis=-1)
        weighted_total = weighted_total * reduce_factor[..., None] + jnp.einsum(
            "rkgj,jkd->rkgd",
            weights.astype(jnp.bfloat16),
            block_values,
            preferred_element_type=jnp.float32,
        )
        return ((new_max, totals, weighted_total), None)

    carried = start_carry
    rows_per_shard = lax.all_gather(cache_key_value, "ctx", axis=1, tiled=True)
    count_of_keys = rows_per_shard.shape[1]
    key_extent = 512
    piled_outputs = rows_per_shard.reshape(
        2, count_of_keys // key_extent, key_extent, KEY_VALUE_HEADS, HEAD_SIZE
    )
    carried, unused = lax.scan(absorb_block, carried, (piled_outputs[0], piled_outputs[1]))
    running_max, totals, weighted_total = carried
    attention = (
        (weighted_total / totals[..., None])
        .reshape(count_of_rows, QUERY_HEADS * HEAD_SIZE)
        .astype(jnp.bfloat16)
    )
    projected = jnp.dot(
        attention,
        lax.all_gather(out_proj, "ctx", axis=0, tiled=True),
        preferred_element_type=jnp.float32,
    )
    hidden = (residual.astype(jnp.float32) + projected).astype(jnp.bfloat16)
    hidden_wide = hidden.astype(jnp.float32)
    normed = (
        hidden_wide
        * lax.rsqrt(jnp.mean(hidden_wide * hidden_wide, axis=-1, keepdims=True) + epsilon)
        * norm_gain
    ).astype(jnp.bfloat16)
    expert_count = placement.shape[0]
    capacity = max(2, 3 * count_of_rows * TOPK // (2 * expert_count))
    expert_range = jnp.arange(expert_count, dtype=jnp.int32)
    slot_ids = jnp.sum(
        jnp.where(route_ids[..., None] == expert_range, placement, 0), axis=-1
    ).reshape(-1)
    assigned = count_of_rows * TOPK
    one_hot = (slot_ids[:, None] == expert_range[None, :]).astype(jnp.int32)
    ranks = jnp.sum(one_hot * (jnp.cumsum(one_hot, axis=0) - 1), axis=1)
    target = slot_ids * capacity + ranks
    source = (
        jnp.full((expert_count * capacity,), assigned, jnp.int32)
        .at[target]
        .set(jnp.arange(assigned, dtype=jnp.int32))
    )
    filled = source < assigned
    source_rows = jnp.minimum(source // TOPK, count_of_rows - 1)
    outgoing = jnp.where(filled[:, None], normed[source_rows], jnp.zeros((), jnp.bfloat16)).reshape(
        expert_count, capacity, D
    )
    incoming = lax.all_to_all(outgoing, "ctx", split_axis=0, concat_axis=0, tiled=True)
    local_count = w_gate_up.shape[0]
    grouped = incoming.reshape(-1, local_count, capacity, D)
    both = jnp.einsum("nemd,edf->nemf", grouped, w_gate_up, preferred_element_type=jnp.float32)
    active = (jax.nn.silu(both[..., :FF]) * both[..., FF:]).astype(jnp.bfloat16)
    produced = jnp.einsum(
        "nemf,efd->nemd", active, w_down, preferred_element_type=jnp.float32
    ).astype(jnp.bfloat16)
    returned = lax.all_to_all(
        produced.reshape(expert_count, capacity, D), "ctx", split_axis=0, concat_axis=0, tiled=True
    )
    routed = (
        returned.reshape(expert_count * capacity, D)[target]
        .reshape(count_of_rows, TOPK, D)
        .astype(jnp.float32)
    )
    gate_share = route_weights / jnp.sum(route_weights, axis=-1, keepdims=True)
    expert_out = jnp.sum(gate_share[..., None] * routed, axis=1).astype(jnp.bfloat16)
    return (hidden, expert_out)


def solution(mesh):
    in_specs = (
        P(("groups", "ctx"), None),
        P(None, ("groups", "ctx"), None),
        P(None, ("groups", "ctx"), None),
        P(("groups", "ctx"), None),
        P(),
        P("ctx", None),
        P("ctx", None, None),
        P("ctx", None, None),
        P(("groups", "ctx"), None),
        P(("groups", "ctx"), None),
        P(),
    )
    out_specs = (P(("groups", "ctx"), None), P(("groups", "ctx"), None))
    return jax.shard_map(local, mesh=mesh, in_specs=in_specs, out_specs=out_specs, check_vma=False)
```

profile of v0, /device:TPU:13, one launch (start us, length us, event | category | flops | bytes accessed | tf_op | source)
XLA Modules:
  0.0 444.1 jit_solution(2338805867204558841)
XLA Ops:
  7.2 0.7 all-gather.3.cloned.1.call-update
  7.9 0.7 all-gather.5.cloned.1.call-update
  8.7 0.8 select_reduce_fusion
  9.7 1.2 copy.67
  10.9 0.9 slice_convert_fusion
  12.2 0.5 fusion.47
  12.9 1.5 reduce-window.6
  15.0 4.1 scatter_custom_fusion
  19.3 42.0 %all-gather.3.cloned.1.call-done = bf16[2,2048,512]{2,1,0:T(8,128)(2,1)} async-done(((bf16[2,128,512]{2,1,0:T(8,128)(2,1)}), bf16[2,2048,512]{2,1,0:T(8,128)(2,1)}) %all-gather.3.cloned.1.call-update) | async-done | bytes 4194320 | tf_op jit(solution)/shard_map/all_gather | solution.py:68
  61.2 3.9 fusion.46
  65.1 4.0 squeeze.13
  69.1 2.1 squeeze.14
  71.3 39.0 %while.15 = (s32[]{:T(128)}, f32[80,4,8]{0,2,1:T(8,128)S(1)}, f32[80,4,8]{0,2,1:T(8,128)S(1)}, f32[80,4,8,128]{3,0,2,1:T(8,128)S(1)}, bf16[4,512,4,128]{3,2,1,0:...) while((s32[]{:T(128)}, f32[80,4,8]{0,2,1:T(8,128)S(1)}, ...), condition=%wide.region_3.4_spmd.clone, body=%wide.region_0.3_spmd.clone.sunk | while | flops 682237440 | bytes 43286664 | solution.py:74
  71.3 1.7 constant_dynamic-slice_fusion.3
  73.0 0.9 bitcast_reduce_fusion.2
  74.0 2.3 copy-done
  76.3 1.5 fusion.59
  77.8 3.3 fusion.61
  81.2 1.6 constant_dynamic-slice_fusion.3
  82.7 0.9 bitcast_reduce_fusion.2
  83.7 2.3 copy-done
  86.0 1.5 fusion.59
  87.5 3.4 fusion.61
  90.9 1.6 constant_dynamic-slice_fusion.3
  92.5 0.9 bitcast_reduce_fusion.2
  93.5 2.3 copy-done
  95.8 1.5 fusion.59
  97.3 3.3 fusion.61
  100.7 1.6 constant_dynamic-slice_fusion.3
  102.2 0.9 bitcast_reduce_fusion.2
  103.2 2.3 copy-done
  105.5 1.5 fusion.59
  107.0 3.3 fusion.61
  110.4 0.4 divide_convert_fusion
  111.0 75.7 %all-gather.5.cloned.1.call-done = bf16[4096,2048]{1,0:T(8,128)(2,1)} async-done(((bf16[256,2048]{1,0:T(8,128)(2,1)}), bf16[4096,2048]{1,0:T(8,128)(2,1)}) %all-gather.5.cloned.1.call-update) | async-done | bytes 16777232 | tf_op jit(solution)/shard_map/all_gather | solution.py:83
  186.6 8.9 %fusion.31 = (f32[80]{0:T(128)S(1)}, bf16[80,2048]{1,0:T(8,128)(2,1)S(1)}) fusion(bf16[4096,2048]{1,0:T(8,128)(2,1)} %all-gather.5.cloned.1.call-done, bf16[10,8,32,128]{3,2,1,0:T(8,128)(2,1)S(1)} %bitcast.103, bf16[80,2048]{1,0:T(8,128)(2,1)S(1)} %copy-done.2), kind=kOutput, calls=%fused_computation.40 | convolution fusion | flops 1343160192 | bytes 18088256 | tf_op jit(solution)/shard_map/dot_general | solution.py:81
  195.7 5.9 %gather_fusion = bf16[960,2048]{1,0:T(8,128)(2,1)} fusion(bf16[80,2048]{1,0:T(8,128)(2,1)S(1)} %fusion.33, s32[1024]{0:T(1024)S(1)} %pad_clamp_fusion.1), kind=kCustom, calls=%fused_computation | custom fusion | bytes 7868160 | tf_op jit(solution)/shard_map/gather | solution.py:110
  201.6 5.0 %gather.9 = bf16[32,30,2048]{2,1,0:T(8,128)(2,1)} reshape(bf16[960,2048]{1,0:T(8,128)(2,1)} %gather_fusion) | data formatting | bytes 7864320 | tf_op jit(solution)/shard_map/gather | solution.py:110
  206.6 2.5 broadcast_select_fusion
  209.2 98.1 %all_to_all.10 = bf16[32,30,2048]{2,1,0:T(8,128)(2,1)S(1)} all-to-all(bf16[32,30,2048]{2,1,0:T(8,128)(2,1)S(1)} %broadcast_select_fusion), channel_id=1, replica_groups=mesh['groups'=2,'ctx'=16] {'ctx'}, dimensions={0} | all-to-all | bytes 7864320 | tf_op jit(solution)/shard_map/all_to_all | solution.py:113
  307.3 9.5 %fusion.21 = f32[16,2,30,1536]{3,2,0,1:T(8,128)S(1)} fusion(bf16[2,2048,1536]{2,1,0:T(8,128)(2,1)} %param.19, bf16[16,2,30,2048]{3,2,1,0:T(8,128)(2,1)S(1)} %bitcast.102), kind=kOutput, calls=%fused_computation.28 | convolution fusion | flops 6039797760 | bytes 22413312 | tf_op jit(solution)/shard_map/nemd,edf->nemf/dot_general | solution.py:116
  316.8 3.8 convert_bitcast_fusion
  320.6 2.3 copy.62
  322.9 5.0 %all-to-all-start.1 = ((bf16[32,30,2048]{2,1,0:T(8,128)(2,1)}), bf16[32,30,2048]{2,1,0:T(8,128)(2,1)}, u32[]{:S(2)}, u32[]{:S(2)}) async-start(bf16[32,30,2048]{2,1,0:T(8,128)(2,1)} %bitcast.101), calls=%async_computation.1 | async-start | bytes 8388608 | tf_op jit(solution)/shard_map/all_to_all | solution.py:121
  328.0 92.3 %all-to-all-done.1 = bf16[32,30,2048]{2,1,0:T(8,128)(2,1)} async-done(((bf16[32,30,2048]{2,1,0:T(8,128)(2,1)}), bf16[32,30,2048]{2,1,0:T(8,128)(2,1)}, u32[]{:S(2)}, u32[]{:S(2)}) %all-to-all-start.1) | async-done | bytes 3932192 | tf_op jit(solution)/shard_map/all_to_all | solution.py:121
  420.3 5.0 %reshape.108 = bf16[960,2048]{1,0:T(8,128)(2,1)} reshape(bf16[32,30,2048]{2,1,0:T(8,128)(2,1)} %all-to-all-done.1) | data formatting | bytes 7864320 | tf_op jit(solution)/shard_map/reshape | solution.py:125
  425.3 9.0 %gather_fusion.1 = bf16[640,2048]{1,0:T(8,128)(2,1)S(1)} fusion(bf16[960,2048]{1,0:T(8,128)(2,1)} %reshape.108, s32[1024]{0:T(1024)S(1)} %pad_clamp_fusion), kind=kCustom, calls=%fused_computation.1 | custom fusion | bytes 5245440 | tf_op jit(solution)/shard_map/gather | solution.py:125
  434.3 2.9 fusion.20
  (62 shorter events, 2.2 us)
Async XLA Ops:
  7.2 54.1 %all-gather.3.cloned.1.call-start = ((), (), s32[]{:S(2)}) async-start(), calls=%async_computation.2 | async-start | bytes 4456448 | tf_op jit(solution)/shard_map/all_gather | solution.py:68
  7.9 178.7 %all-gather.5.cloned.1.call-start = ((), (), s32[]{:S(2)}) async-start(), calls=%async_computation.3 | async-start | bytes 17825792 | tf_op jit(solution)/shard_map/all_gather | solution.py:83
  71.3 115.3 %copy-start.2 = (bf16[80,2048]{1,0:T(8,128)(2,1)S(1)}, bf16[80,2048]{1,0:T(8,128)(2,1)}, u32[]{:S(2)}) copy-start(bf16[80,2048]{1,0:T(8,128)(2,1)} %param.16) | copy-start | bytes 983044
  74.0 2.3 copy-start
  83.7 2.3 copy-start
  93.4 2.3 copy-start
  103.2 2.3 copy-start
  186.6 8.9 %copy-start.4 = (f32[2048]{0:T(1024)S(1)}, f32[2048]{0:T(1024)}, u32[]{:S(2)}) copy-start(f32[2048]{0:T(1024)} %param.17) | copy-start | bytes 24580
  195.5 6.1 %copy-start.1 = (bf16[80,2048]{1,0:T(8,128)(2,1)}, bf16[80,2048]{1,0:T(8,128)(2,1)S(1)}, u32[]{:S(2)}) copy-start(bf16[80,2048]{1,0:T(8,128)(2,1)S(1)} %get-tuple-element.112) | copy-start | bytes 983044
  209.2 107.6 %slice-start = ((s8[6291456]{0:T(1024)(128)(4,1)}), s8[4194304]{0:T(1024)(128)(4,1)S(1)}, s32[]{:S(2)}) async-start(s8[6291456]{0:T(1024)(128)(4,1)} %bitcast.108), calls=%async_computation.4 | async-start | bytes 8388608
  307.3 9.5 %slice-start.1 = ((s8[6291456]{0:T(1024)(128)(4,1)}), s8[2097152]{0:T(1024)(128)(4,1)S(1)}, s32[]{:S(2)}) async-start(s8[6291456]{0:T(1024)(128)(4,1)} %bitcast.108), calls=%async_computation.5 | async-start | bytes 4194304
  322.9 5.0 %copy-start.3 = (f32[80,8]{0,1:T(8,128)S(1)}, f32[80,8]{0,1:T(8,128)}, u32[]{:S(2)}) copy-start(f32[80,8]{0,1:T(8,128)} %param.22) | copy-start | bytes 7684
  322.9 97.4 %all-to-all-start.1 = ((bf16[32,30,2048]{2,1,0:T(8,128)(2,1)}), bf16[32,30,2048]{2,1,0:T(8,128)(2,1)}, u32[]{:S(2)}, u32[]{:S(2)}) async-start(bf16[32,30,2048]{2,1,0:T(8,128)(2,1)} %bitcast.101), calls=%async_computation.1 | async-start | bytes 8388608 | tf_op jit(solution)/shard_map/all_to_all | solution.py:121
Sparse Core Ops, SparseCore 0:
  10.2 51.0 all-gather.2
  63.4 123.1 all-gather.4
where the time goes:
time: 445 us; the launch traced here: 444 us
  waiting for transfers between devices  211 us (47%)
  blocking collectives  98.1 us (22%)
  local copies, waits for them, and re-layouts  59.7 us (13%)
  matrix products  39.7 us (9%)
  other arithmetic  15.5 us (3%)
  between operations  14.3 us (3%)
  starting transfers between devices  5.04 us (1%)
    all_to_all x1, blocking collectives, local(): lax.all_to_all(outgoing, 'ctx', split_axis=0, concat_axis=0, tiled=True)  98.1 us
    all_to_all x1, waiting for transfers between devices, local(): lax.all_to_all(produced.reshape(expert_count, capacity, D), 'ctx', split_...  92.3 us
    all_gather x1, waiting for transfers between devices, local(): lax.all_gather(out_proj, 'ctx', axis=0, tiled=True)  75.7 us
    all_gather x1, waiting for transfers between devices, local(): rows_per_shard = lax.all_gather(cache_key_value, 'ctx', axis=1, tiled=True)  42 us
    dot_general x4, matrix products, absorb_block(): jnp.einsum('rkgj,jkd->rkgd', weights.astype(jnp.bfloat16), block_values,...  13.4 us
    gather x2, local copies, waits for them, and re-layouts, local(): normed[source_rows]  10.9 us
    dot_general x1, matrix products, local(): jnp.einsum('nemd,edf->nemf', grouped, w_gate_up, preferred_element_type=j...  9.47 us
    while x12, local copies, waits for them, and re-layouts  9.2 us
  transfers between devices with their start and end apart: 3, of which 3 were waited for; matrix products, arithmetic and copies ran while one was open for 11% of the time, Pallas kernels for 0%

commit v1 on v0

v1 whole, which is shorter than its diff:
```python
import functools

import jax
import jax.numpy as jnp
from jax import lax
from jax.experimental import pallas as pl
from jax.experimental.pallas import tpu as pltpu
from jax.sharding import PartitionSpec as P

D = 2048
QUERY_HEADS = 32
KEY_VALUE_HEADS = 4
HEAD_SIZE = 128
FF = 768
TOPK = 8
HEADS_STEP = 4

epsilon = 1e-06

VMEM = pl.BlockSpec(memory_space=pltpu.VMEM)
RIGHT, LEFT = 0, 1


def chip_at(q, m):
    return jnp.where(q < m // 2, 2 * q, 2 * (m - 1 - q) + 1)


def place_of(chip, m):
    return jnp.where(chip % 2 == 0, chip // 2, m - 1 - chip // 2)


def ring(m):
    me = lax.axis_index("ctx")
    core, p = me % 2, place_of(me // 2, m)

    def at(offset, c):
        return chip_at((p + offset + m) % m, m) * 2 + c

    return me, core, at


def greet(others):
    barrier = pltpu.get_barrier_semaphore()
    for other in others:
        pl.semaphore_signal(
            barrier, inc=1, device_id={"ctx": other}, device_id_type=pl.DeviceIdType.MESH
        )
    pl.semaphore_wait(barrier, len(others))


def remote(src, dst, send, recv, other):
    return pltpu.make_async_remote_copy(
        src_ref=src,
        dst_ref=dst,
        send_sem=send,
        recv_sem=recv,
        device_id={"ctx": other},
        device_id_type=pl.DeviceIdType.MESH,
    )


def travels(way, half, d, reach):
    return d < reach or (d == reach and half == way)


PAIRS = ((RIGHT, 0), (LEFT, 1), (RIGHT, 1), (LEFT, 0))


def gather_kernel(n, x_ref, out_ref, ring_send, ring_recv, mate_send, mate_recv):
    m, reach = n // 2, n // 4
    me, core, at = ring(m)
    mate = at(0, 1 - core)
    neighbour = (at(1, core), at(-1, core))
    half_width = x_ref.shape[1] // 2
    cols = [pl.ds(h * half_width, half_width) for h in range(2)]
    greet((neighbour[0], neighbour[1], mate))
    started = []

    def forward(src, owner, way, half, d):
        copy = remote(
            src,
            out_ref.at[owner, :, cols[half]],
            ring_send.at[way, d, half],
            ring_recv.at[way, d, half],
            neighbour[way],
        )
        copy.start()
        started.append(copy)

    for way, half in PAIRS:
        forward(x_ref.at[:, cols[half]], me, way, half, 0)
    copy = remote(x_ref, out_ref.at[me], mate_send.at[0, 0, 0], mate_recv.at[0, 0, 0], mate)
    copy.start()
    started.append(copy)
    out_ref[me] = x_ref[...]
    for d in range(1, reach + 1):
        for way, half in PAIRS:
            if not travels(way, half, d, reach):
                continue
            owner = at(-d if way == RIGHT else d, core)
            piece = out_ref.at[owner, :, cols[half]]
            remote(
                piece, piece, ring_send.at[way, d - 1, half], ring_recv.at[way, d - 1, half], mate
            ).wait_recv()
            if travels(way, half, d + 1, reach):
                forward(piece, owner, way, half, d)
            copy = remote(
                piece, piece, mate_send.at[way, d, half], mate_recv.at[way, d, half], mate
            )
            copy.start()
            started.append(copy)
    theirs = out_ref.at[mate]
    remote(theirs, theirs, mate_send.at[0, 0, 0], mate_recv.at[0, 0, 0], mate).wait_recv()
    for d in range(1, reach + 1):
        for way, half in PAIRS:
            if travels(way, half, d, reach):
                owner = at(-d if way == RIGHT else d, 1 - core)
                piece = out_ref.at[owner, :, cols[half]]
                remote(
                    piece, piece, mate_send.at[way, d, half], mate_recv.at[way, d, half], mate
                ).wait_recv()
    for copy in started:
        copy.wait_send()


def ring_gather(x, n, collective_id):
    reach = n // 4
    return pl.pallas_call(
        functools.partial(gather_kernel, n),
        out_shape=jax.ShapeDtypeStruct((n,) + x.shape, x.dtype),
        in_specs=[VMEM],
        out_specs=VMEM,
        scratch_shapes=[
            pltpu.SemaphoreType.DMA((2, reach, 2)),
            pltpu.SemaphoreType.DMA((2, reach, 2)),
            pltpu.SemaphoreType.DMA((2, reach + 1, 2)),
            pltpu.SemaphoreType.DMA((2, reach + 1, 2)),
        ],
        compiler_params=pltpu.CompilerParams(collective_id=collective_id, has_side_effects=True),
        name=f"gather{collective_id}",
    )(x)


def scatter_kernel(
    n,
    x_ref,
    out_ref,
    from_mate,
    outgoing,
    incoming,
    ring_send,
    ring_recv,
    mate_send,
    mate_recv,
):
    m, reach = n // 2, n // 4
    me, core, at = ring(m)
    mate = at(0, 1 - core)
    neighbour = (at(1, core), at(-1, core))
    half_width = x_ref.shape[2] // 2
    cols = [pl.ds(h * half_width, half_width) for h in range(2)]
    greet((neighbour[0], neighbour[1], mate))
    started = []
    offsets = [reach]
    for d in range(reach - 1, 0, -1):
        offsets += [d, -d]
    offsets.append(0)
    mate_copies = []
    for k, offset in enumerate(offsets):
        copy = remote(
            x_ref.at[at(offset, 1 - core)],
            from_mate.at[k],
            mate_send.at[k],
            mate_recv.at[k],
            mate,
        )
        copy.start()
        started.append(copy)
        mate_copies.append(copy)
    arrived = set()

    def chip_sum(offset, half):
        k = offsets.index(offset)
        if k not in arrived:
            mate_copies[k].wait_recv()
            arrived.add(k)
        mine = x_ref[at(offset, core), :, cols[half]].astype(jnp.float32)
        return mine + from_mate[k, :, cols[half]].astype(jnp.float32)

    def received(way, half, d):
        piece = incoming.at[way, d, half]
        remote(
            piece, piece, ring_send.at[way, d, half], ring_recv.at[way, d, half], mate
        ).wait_recv()
        return incoming[way, d, half].astype(jnp.float32)

    for d in range(reach, 0, -1):
        for way, half in ((RIGHT, 1), (LEFT, 0), (RIGHT, 0), (LEFT, 1)):
            if not travels(way, half, d, reach):
                continue
            offset = d if (way == RIGHT or d == reach) else -d
            total = chip_sum(offset, half)
            if travels(way, half, d + 1, reach):
                total = total + received(way, half, d)
            outgoing[way, d - 1, half] = total.astype(jnp.bfloat16)
            copy = remote(
                outgoing.at[way, d - 1, half],
                incoming.at[way, d - 1, half],
                ring_send.at[way, d - 1, half],
                ring_recv.at[way, d - 1, half],
                neighbour[way],
            )
            copy.start()
            started.append(copy)
    for half in range(2):
        total = chip_sum(0, half) + received(RIGHT, half, 0) + received(LEFT, half, 0)
        out_ref[:, cols[half]] = total
    for copy in started:
        copy.wait_send()


def ring_scatter(x, n, collective_id):
    m, reach = n // 2, n // 4
    rows, width = x.shape[1:]
    piece = (2, reach, 2, rows, width // 2)
    return pl.pallas_call(
        functools.partial(scatter_kernel, n),
        out_shape=jax.ShapeDtypeStruct((rows, width), jnp.float32),
        in_specs=[VMEM],
        out_specs=VMEM,
        scratch_shapes=[
            pltpu.VMEM((m, rows, width), jnp.bfloat16),
            pltpu.VMEM(piece, jnp.bfloat16),
            pltpu.VMEM(piece, jnp.bfloat16),
            pltpu.SemaphoreType.DMA((2, reach, 2)),
            pltpu.SemaphoreType.DMA((2, reach, 2)),
            pltpu.SemaphoreType.DMA((m,)),
            pltpu.SemaphoreType.DMA((m,)),
        ],
        compiler_params=pltpu.CompilerParams(collective_id=collective_id, has_side_effects=True),
        name=f"scatter{collective_id}",
    )(x)


def exchange_kernel(n, x_ref, out_ref, send, recv):
    me = lax.axis_index("ctx")
    greet([(me + j) % n for j in range(1, n)])
    copies = []
    for j in range(1, n):
        other = (me + j) % n
        copy = remote(x_ref.at[other], out_ref.at[me], send.at[j], recv.at[j], other)
        copy.start()
        copies.append(copy)
    out_ref[me] = x_ref[me]
    for j in range(1, n):
        source = (me + n - j) % n
        piece = out_ref.at[source]
        remote(piece, piece, send.at[j], recv.at[j], source).wait_recv()
    for copy in copies:
        copy.wait_send()


def exchange(x, n, collective_id):
    return pl.pallas_call(
        functools.partial(exchange_kernel, n),
        out_shape=jax.ShapeDtypeStruct(x.shape, x.dtype),
        in_specs=[VMEM],
        out_specs=VMEM,
        scratch_shapes=[pltpu.SemaphoreType.DMA((n,)), pltpu.SemaphoreType.DMA((n,))],
        compiler_params=pltpu.CompilerParams(collective_id=collective_id, has_side_effects=True),
        name=f"exchange{collective_id}",
    )(x)


def attend_kernel(per, q_ref, fresh_key_ref, fresh_value_ref, key_ref, value_ref, out_ref):
    rows = q_ref.shape[0]
    keys = key_ref[...].reshape(-1, HEAD_SIZE)
    values = value_ref[...].reshape(-1, HEAD_SIZE)
    fresh_key = fresh_key_ref[...].astype(jnp.float32)
    fresh_value = fresh_value_ref[...].astype(jnp.float32)
    scale = HEAD_SIZE ** (-0.5)
    heads = [q_ref[:, h * HEAD_SIZE : (h + 1) * HEAD_SIZE] for h in range(HEADS_STEP)]
    scores = (
        lax.dot_general(
            jnp.concatenate(heads, axis=0),
            keys,
            (((1,), (1,)), ((), ())),
            preferred_element_type=jnp.float32,
        )
        * scale
    )
    own = jnp.concatenate(
        [jnp.sum(q.astype(jnp.float32) * fresh_key, axis=-1, keepdims=True) for q in heads], axis=0
    )
    own = own * scale
    peak = jnp.maximum(own, jnp.max(scores, axis=-1, keepdims=True))
    weights = jnp.exp(scores - peak)
    own = jnp.exp(own - peak)
    totals = jnp.sum(weights, axis=-1, keepdims=True) + own
    mixed = jnp.dot(weights.astype(jnp.bfloat16), values, preferred_element_type=jnp.float32)
    for h in range(HEADS_STEP):
        part = slice(h * rows, (h + 1) * rows)
        result = (mixed[part] + own[part] * fresh_value) / totals[part]
        column = (h % per) * HEAD_SIZE
        out_ref[h // per, :, column : column + HEAD_SIZE] = result.astype(jnp.bfloat16)


def attend(queries, fresh_key_value, gathered, key_count, n):
    rows = queries.shape[0]
    per = QUERY_HEADS // n
    parts = QUERY_HEADS // KEY_VALUE_HEADS // HEADS_STEP
    fresh = lambda i: pl.BlockSpec((None, rows, HEAD_SIZE), lambda g, s, i=i: (i, 0, g))
    cached = lambda i: pl.BlockSpec((n, key_count, HEAD_SIZE), lambda g, s, i=i: (0, i, g))
    return pl.pallas_call(
        functools.partial(attend_kernel, per),
        grid=(KEY_VALUE_HEADS, parts),
        out_shape=jax.ShapeDtypeStruct((n, rows, per * HEAD_SIZE), jnp.bfloat16),
        in_specs=[
            pl.BlockSpec((rows, HEADS_STEP * HEAD_SIZE), lambda g, s: (0, g * parts + s)),
            fresh(0),
            fresh(1),
            cached(0),
            cached(1),
        ],
        out_specs=pl.BlockSpec(
            (HEADS_STEP // per, rows, per * HEAD_SIZE), lambda g, s: (g * parts + s, 0, 0)
        ),
        name="attend",
    )(queries, fresh_key_value, fresh_key_value, gathered, gathered)


def local(
    n,
    queries,
    fresh_key_value,
    cache_key_value,
    residual,
    norm_gain,
    out_proj,
    w_gate_up,
    w_down,
    route_ids,
    route_weights,
    placement,
):
    rows = queries.shape[0]
    expert_count = placement.shape[0]
    local_count = w_gate_up.shape[0]
    key_count = cache_key_value.shape[1]
    kv_width = cache_key_value.shape[2]
    capacity = n * max(2, 3 * rows * TOPK // (2 * expert_count))

    gate_share = route_weights / jnp.sum(route_weights, axis=-1, keepdims=True)
    slots = jnp.sum(
        jnp.where(route_ids[..., None] == jnp.arange(expert_count), placement, 0), axis=-1
    )
    slot_lanes = -(-expert_count // 128) * 128
    shares = jnp.sum(
        jnp.where(slots[..., None] == jnp.arange(slot_lanes), gate_share[..., None], 0.0), axis=1
    ).astype(jnp.bfloat16)
    share_rows = rows * slot_lanes // kv_width
    padded = -(-share_rows // 16) * 16
    packed = jnp.concatenate(
        [
            cache_key_value.reshape(2 * key_count, kv_width),
            jnp.pad(shares.reshape(share_rows, kv_width), ((0, padded - share_rows), (0, 0))),
        ],
        axis=0,
    )
    gathered = ring_gather(packed, n, 0)

    mine = lax.axis_index("ctx") * local_count
    all_shares = gathered[:, 2 * key_count : 2 * key_count + share_rows].reshape(
        n * rows, slot_lanes
    )
    my_shares = lax.dynamic_slice(all_shares, (0, mine), (n * rows, local_count)).T
    named = my_shares > 0
    ranks = jnp.cumsum(named.astype(jnp.int32), axis=1) - 1
    ranks = jnp.where(named, ranks, -1)
    chosen = ranks[:, None, :] == jnp.arange(capacity)[None, :, None]
    pick = chosen.astype(jnp.bfloat16).reshape(local_count * capacity, n * rows)
    spread = jnp.where(chosen, my_shares[:, None, :], jnp.zeros((), jnp.bfloat16)).reshape(
        local_count * capacity, n * rows
    )

    attention = exchange(attend(queries, fresh_key_value, gathered, key_count, n), n, 1)
    projected = jnp.dot(
        attention.reshape(n * rows, -1), out_proj, preferred_element_type=jnp.float32
    ).astype(jnp.bfloat16)
    projected = ring_scatter(projected.reshape(n, rows, D), n, 2)
    hidden = (residual.astype(jnp.float32) + projected).astype(jnp.bfloat16)
    hidden_wide = hidden.astype(jnp.float32)
    normed = (
        hidden_wide
        * lax.rsqrt(jnp.mean(hidden_wide * hidden_wide, axis=-1, keepdims=True) + epsilon)
        * norm_gain
    ).astype(jnp.bfloat16)
    all_normed = ring_gather(normed, n, 3).reshape(n * rows, D)

    inputs = (
        jnp.dot(pick, all_normed, preferred_element_type=jnp.float32)
        .astype(jnp.bfloat16)
        .reshape(local_count, capacity, D)
    )
    both = jnp.einsum("emd,edf->emf", inputs, w_gate_up, preferred_element_type=jnp.float32)
    active = (jax.nn.silu(both[..., :FF]) * both[..., FF:]).astype(jnp.bfloat16)
    produced = jnp.einsum(
        "emf,efd->emd", active, w_down, preferred_element_type=jnp.float32
    ).astype(jnp.bfloat16)
    combined = lax.dot_general(
        spread,
        produced.reshape(local_count * capacity, D),
        (((0,), (0,)), ((), ())),
        preferred_element_type=jnp.float32,
    ).astype(jnp.bfloat16)
    expert_out = ring_scatter(combined.reshape(n, rows, D), n, 4).astype(jnp.bfloat16)
    return (hidden, expert_out)


def solution(mesh):
    in_specs = (
        P(("groups", "ctx"), None),
        P(None, ("groups", "ctx"), None),
        P(None, ("groups", "ctx"), None),
        P(("groups", "ctx"), None),
        P(),
        P("ctx", None),
        P("ctx", None, None),
        P("ctx", None, None),
        P(("groups", "ctx"), None),
        P(("groups", "ctx"), None),
        P(),
    )
    out_specs = (P(("groups", "ctx"), None), P(("groups", "ctx"), None))
    return jax.shard_map(
        functools.partial(local, mesh.shape["ctx"]),
        mesh=mesh,
        in_specs=in_specs,
        out_specs=out_specs,
        check_vma=False,
    )
```

time: 445 us -> 217 us (0.49)
  waiting for transfers between devices: 211 us -> 0 us
  Pallas kernels: 0 us -> 164 us
  blocking collectives: 98.1 us -> 0 us
  local copies, waits for them, and re-layouts: 59.7 us -> 1.62 us
  between operations: 14.3 us -> 0.82 us
  other arithmetic: 15.5 us -> 9.98 us
  starting transfers between devices: 5.04 us -> 0 us
    pallas_call x0 -> x6, Pallas kernels: none -> 164 us  [the longest x2 66.2 us: ring_scatter(): pl.pallas_call(functools.partial(scatter_kernel, n), out_shape=jax.ShapeD...]
    all_gather x2 -> x0, waiting for transfers between devices: 118 us -> none  [the longest x1 75.7 us: local(): lax.all_gather(out_proj, 'ctx', axis=0, tiled=True)]
    all_to_all x1 -> x0, blocking collectives: 98.1 us -> none  [local(): lax.all_to_all(outgoing, 'ctx', split_axis=0, concat_axis=0, tiled=True)]
    all_to_all x1 -> x0, waiting for transfers between devices: 92.3 us -> none  [local(): lax.all_to_all(produced.reshape(expert_count, capacity, D), 'ctx', split_...]
    gather x3 -> x0, local copies, waits for them, and re-layouts: 19.9 us -> none  [the longest x2 10.9 us: local(): normed[source_rows]]
    while x12 -> x0, local copies, waits for them, and re-layouts: 9.2 us -> none
    reduce_sum x7 -> x3, other arithmetic: 9.8 us -> 2.34 us  [the longest x1 1.28 us: local(): jnp.mean(hidden_wide * hidden_wide, axis=-1, keepdims=True) + epsilon]
    reshape x2 -> x1, local copies, waits for them, and re-layouts: 7.28 us -> 0.21 us  [local(): gathered[:, 2 * key_count:2 * key_count + share_rows]]
  transfers between devices with their start and end apart: 3 -> 0, of which waited for: 3 -> 0; matrix products, arithmetic and copies ran while one was open for 11% -> 0% of each run, Pallas kernels for 0% -> 0%
where the time goes in v1:
time: 217 us; the launch traced here: 213 us
  Pallas kernels  164 us (76%)
  matrix products  36.9 us (17%)
  other arithmetic  9.98 us (5%)
    pallas_call x2, Pallas kernels, ring_scatter(): pl.pallas_call(functools.partial(scatter_kernel, n), out_shape=jax.ShapeD...  66.2 us
    pallas_call x2, Pallas kernels, ring_gather(): pl.pallas_call(functools.partial(gather_kernel, n), out_shape=jax.ShapeDt...  64 us
    pallas_call x1, Pallas kernels, exchange(): pl.pallas_call(functools.partial(exchange_kernel, n), out_shape=jax.Shape...  19.7 us
    pallas_call x1, Pallas kernels, attend(): pl.pallas_call(functools.partial(attend_kernel, per), grid=(KEY_VALUE_HEA...  14.3 us
    dot_general x1, matrix products, local(): lax.dot_general(spread, produced.reshape(local_count * capacity, D), (((0...  14.2 us
    dot_general x1, matrix products, local(): jnp.einsum('emd,edf->emf', inputs, w_gate_up, preferred_element_type=jnp....  10.9 us
    dot_general x1, matrix products, local(): jnp.dot(pick, all_normed, preferred_element_type=jnp.float32)  7.94 us

profile of v1, /device:TPU:13, one launch (start us, length us, event | category | flops | bytes accessed | tf_op | source)
XLA Modules:
  0.0 213.4 jit_solution(6068265124650075543)
XLA Ops:
  0.6 0.0 copy-start
  0.6 0.8 reduce_sum.37
  1.4 0.7 broadcast_divide_fusion
  2.1 0.8 select_reduce_fusion.1
  2.9 0.1 copy.25
  3.0 0.1 copy.26
  3.1 0.3 select_reduce_fusion
  3.4 1.7 fusion.17.x_ref
  5.1 31.2 %gather0.1.key_ref.value_ref = bf16[16,288,512]{2,1,0:T(8,128)(2,1)} custom-call(bf16[288,512]{1,0:T(8,128)(2,1)} %fusion.17.x_ref), custom_call_target="tpu_custom_call" | custom-call | tf_op jit(solution)/shard_map/gather0/pallas_call | solution.py:128
  36.3 0.0 slice-start
  36.3 14.3 %attend.1.x_ref = bf16[16,80,256]{2,1,0:T(8,128)(2,1)} custom-call(bf16[80,4096]{1,0:T(8,128)(2,1)} %q_ref.1, bf16[2,80,512]{2,1,0:T(8,128)(2,1)} %fresh_value_ref.1, bf16[2,80,512]{2,1,0:T(8,128)(2,1)} %fresh_value_ref.1, bf16[16,288,512]{2,1,0:T(8,128)(2,1)} %gather0.1.key_ref.value_ref, bf16[16,288,512]{2,1,0:T(8,128)(2,1)} %gather0.1.key_ref.value_ref), custom_call_target="tpu_custom_call" | custom-call | tf_op jit(solution)/shard_map/attend/pallas_call | solution.py:314
  50.6 0.0 slice-done
  50.6 0.2 reshape.94
  50.9 19.7 %exchange1.1 = bf16[16,80,256]{2,1,0:T(8,128)(2,1)} custom-call(bf16[16,80,256]{2,1,0:T(8,128)(2,1)} %attend.1.x_ref), custom_call_target="tpu_custom_call" | custom-call | tf_op jit(solution)/shard_map/exchange1/pallas_call | solution.py:264
  70.5 0.0 copy-start.1
  70.5 0.2 compare_convert_fusion
  70.7 0.3 copy.31
  71.0 0.6 reduce-window.6
  71.6 0.2 slice_reduce_fusion
  71.8 0.2 reduce-window.9
  72.0 0.1 add_add_fusion
  72.0 0.2 copy.30
  72.2 0.3 copy.32
  72.5 0.1 bitcast_select_fusion
  72.6 0.2 copy.29
  72.8 0.7 iota_compare_fusion
  73.5 0.0 copy-done
  73.5 0.0 copy-done.1
  73.5 3.8 %convolution_convert_fusion = bf16[1280,2048]{1,0:T(8,128)(2,1)} fusion(bf16[1280,256]{1,0:T(8,128)(2,1)S(1)} %bitcast.26, bf16[256,2048]{1,0:T(8,128)(2,1)S(1)} %copy-done), kind=kOutput, calls=%fused_computation.1 | convolution fusion | flops 1344798720 | bytes 6946816 | tf_op jit(solution)/shard_map/dot_general | solution.py:387
  77.3 0.0 copy-start.3
  77.4 0.0 copy-start.4
  77.4 33.7 %scatter2.1 = f32[80,2048]{1,0:T(8,128)} custom-call(bf16[16,80,2048]{2,1,0:T(8,128)(2,1)} %bitcast.23), custom_call_target="tpu_custom_call" | custom-call | tf_op jit(solution)/shard_map/scatter2/pallas_call | solution.py:226
  111.1 0.0 copy-done.3
  111.1 1.3 fusion.13
  112.4 0.0 copy-start.2
  112.4 0.0 copy-done.4
  112.4 0.9 fusion.15.x_ref
  113.3 32.8 %gather3.1 = bf16[16,80,2048]{2,1,0:T(8,128)(2,1)} custom-call(bf16[80,2048]{1,0:T(8,128)(2,1)} %fusion.15.x_ref), custom_call_target="tpu_custom_call" | custom-call | tf_op jit(solution)/shard_map/gather3/pallas_call | solution.py:128
  146.0 7.9 %convolution_convert_fusion.1 = bf16[960,2048]{1,0:T(8,128)(2,1)S(1)} fusion(pred[960,1280]{1,0:T(32,128)(4,1)S(1)} %bitcast.28, bf16[1280,2048]{1,0:T(8,128)(2,1)} %bitcast.25), kind=kOutput, calls=%fused_computation.4 | convolution fusion | flops 5035130880 | bytes 10403840 | tf_op jit(solution)/shard_map/dot_general | solution.py:401
  154.0 0.0 copy-done.2
  154.0 10.9 %fusion.21 = f32[2,480,1536]{2,1,0:T(8,128)} fusion(bf16[2,480,2048]{2,1,0:T(8,128)(2,1)S(1)} %bitcast.31, bf16[2,2048,1536]{2,1,0:T(8,128)(2,1)} %param.17), kind=kOutput, calls=%fused_computation.34 | convolution fusion | flops 6039797760 | bytes 22413312 | tf_op jit(solution)/shard_map/emd,edf->emf/dot_general | solution.py:405
  164.9 14.2 %bitcast_convert_fusion = bf16[1280,2048]{1,0:T(8,128)(2,1)} fusion(bf16[2,768,2048]{2,1,0:T(8,128)(2,1)} %param.18, f32[2,480,1536]{2,1,0:T(8,128)} %fusion.21, bf16[2,1280]{1,0:T(2,128)(2,1)S(1)} %copy.30, s32[2,1280]{1,0:T(2,128)S(1)} %copy.29), kind=kOutput, calls=%fused_computation | convolution fusion | flops 8064532480 | bytes 17447936 | tf_op jit(solution)/shard_map/dot_general | solution.py:410
  179.1 32.5 %scatter4.1 = f32[80,2048]{1,0:T(8,128)} custom-call(bf16[16,80,2048]{2,1,0:T(8,128)(2,1)} %bitcast.24), custom_call_target="tpu_custom_call" | custom-call | tf_op jit(solution)/shard_map/scatter4/pallas_call | solution.py:226
  211.6 1.8 convert_element_type.52
  (2 shorter events, 0.0 us)
Async XLA Ops:
  0.6 72.9 %copy-start = (bf16[256,2048]{1,0:T(8,128)(2,1)S(1)}, bf16[256,2048]{1,0:T(8,128)(2,1)}, u32[]{:S(2)}) copy-start(bf16[256,2048]{1,0:T(8,128)(2,1)} %param.16) | copy-start | bytes 3145732
  36.3 14.3 %slice-start = ((bf16[16,288,512]{2,1,0:T(8,128)(2,1)}), bf16[16,20,512]{2,1,0:T(8,128)(2,1)S(1)}, s32[]{:S(2)}) async-start(bf16[16,288,512]{2,1,0:T(8,128)(2,1)} %gather0.1.key_ref.value_ref), calls=%async_computation | async-start | bytes 786432 | tf_op jit(solution)/shard_map/slice | solution.py:373
  70.5 3.0 %copy-start.1 = (bf16[16,80,256]{2,1,0:T(8,128)(2,1)S(1)}, bf16[16,80,256]{2,1,0:T(8,128)(2,1)}, u32[]{:S(2)}) copy-start(bf16[16,80,256]{2,1,0:T(8,128)(2,1)} %exchange1.1) | copy-start | bytes 1966084
  77.3 33.7 %copy-start.3 = (bf16[80,2048]{1,0:T(8,128)(2,1)S(1)}, bf16[80,2048]{1,0:T(8,128)(2,1)}, u32[]{:S(2)}) copy-start(bf16[80,2048]{1,0:T(8,128)(2,1)} %param.14) | copy-start | bytes 983044
  77.4 35.0 %copy-start.4 = (f32[2048]{0:T(1024)S(1)}, f32[2048]{0:T(1024)}, u32[]{:S(2)}) copy-start(f32[2048]{0:T(1024)} %param.15) | copy-start | bytes 24580
  112.4 41.6 %copy-start.2 = (bf16[80,2048]{1,0:T(8,128)(2,1)}, bf16[80,2048]{1,0:T(8,128)(2,1)S(1)}, u32[]{:S(2)}) copy-start(bf16[80,2048]{1,0:T(8,128)(2,1)S(1)} %get-tuple-element.3) | copy-start | bytes 983044

commit v2 on v1

--- a/solution.py
+++ b/solution.py
@@ -14,6 +14,7 @@
 FF = 768
 TOPK = 8
 HEADS_STEP = 4
+COLUMNS_STEP = 512
 
 epsilon = 1e-06
 
@@ -141,23 +142,16 @@
     )(x)
 
 
-def scatter_kernel(
-    n,
-    x_ref,
-    out_ref,
-    from_mate,
-    outgoing,
-    incoming,
-    ring_send,
-    ring_recv,
-    mate_send,
-    mate_recv,
-):
+def scatter_kernel(n, finish, extras, lhs_ref, rhs_ref, *refs):
+    extra_refs, refs = refs[:extras], refs[extras:]
+    outs, scratch = refs[:-8], refs[-8:]
+    made, from_mate, outgoing, incoming, ring_send, ring_recv, mate_send, mate_recv = scratch
     m, reach = n // 2, n // 4
     me, core, at = ring(m)
     mate = at(0, 1 - core)
     neighbour = (at(1, core), at(-1, core))
-    half_width = x_ref.shape[2] // 2
+    rows, width = made.shape[2:]
+    half_width = width // 2
     cols = [pl.ds(h * half_width, half_width) for h in range(2)]
     greet((neighbour[0], neighbour[1], mate))
     started = []
@@ -165,18 +159,32 @@
     for d in range(reach - 1, 0, -1):
         offsets += [d, -d]
     offsets.append(0)
-    mate_copies = []
-    for k, offset in enumerate(offsets):
+    mate_copies = {}
+
+    def make(offset):
+        k = offsets.index(offset)
+        lhs = lhs_ref.at[at(offset, 0) // 2]
+
+        @pl.loop(0, width // COLUMNS_STEP)
+        def _(c):
+            part = pl.ds(pl.multiple_of(c * COLUMNS_STEP, COLUMNS_STEP), COLUMNS_STEP)
+            product = jnp.dot(lhs[...], rhs_ref[:, part], preferred_element_type=jnp.float32)
+            product = product.astype(jnp.bfloat16)
+            made[k, 0, :, part] = product[:rows]
+            made[k, 1, :, part] = product[rows:]
+
         copy = remote(
-            x_ref.at[at(offset, 1 - core)],
-            from_mate.at[k],
-            mate_send.at[k],
-            mate_recv.at[k],
-            mate,
+            made.at[k, 1 - core], from_mate.at[k], mate_send.at[k], mate_recv.at[k], mate
         )
         copy.start()
         started.append(copy)
-        mate_copies.append(copy)
+        mate_copies[k] = copy
+
+    def make_level(d):
+        for offset in offsets:
+            if abs(offset) == d:
+                make(offset)
+
     arrived = set()
 
     def chip_sum(offset, half):
@@ -184,7 +192,7 @@
         if k not in arrived:
             mate_copies[k].wait_recv()
             arrived.add(k)
-        mine = x_ref[at(offset, core), :, cols[half]].astype(jnp.float32)
+        mine = made[k, core, :, cols[half]].astype(jnp.float32)
         return mine + from_mate[k, :, cols[half]].astype(jnp.float32)
 
     def received(way, half, d):
@@ -194,7 +202,9 @@
         ).wait_recv()
         return incoming[way, d, half].astype(jnp.float32)
 
+    make_level(reach)
     for d in range(reach, 0, -1):
+        make_level(d - 1)
         for way, half in ((RIGHT, 1), (LEFT, 0), (RIGHT, 0), (LEFT, 1)):
             if not travels(way, half, d, reach):
                 continue
@@ -212,23 +222,46 @@
             )
             copy.start()
             started.append(copy)
-    for half in range(2):
-        total = chip_sum(0, half) + received(RIGHT, half, 0) + received(LEFT, half, 0)
-        out_ref[:, cols[half]] = total
+    totals = [
+        chip_sum(0, half) + received(RIGHT, half, 0) + received(LEFT, half, 0) for half in range(2)
+    ]
+    finish(totals, cols, extra_refs, outs)
     for copy in started:
         copy.wait_send()
 
 
-def ring_scatter(x, n, collective_id):
+def finish_plain(totals, cols, extra_refs, outs):
+    for half in range(2):
+        outs[0][:, cols[half]] = totals[half].astype(jnp.bfloat16)
+
+
+def finish_normed(totals, cols, extra_refs, outs):
+    residual_ref, gain_ref = extra_refs
+    hidden_ref, normed_ref = outs
+    squares = 0.0
+    for half in range(2):
+        hidden = totals[half] + residual_ref[:, cols[half]].astype(jnp.float32)
+        hidden = hidden.astype(jnp.bfloat16)
+        hidden_ref[:, cols[half]] = hidden
+        wide = hidden.astype(jnp.float32)
+        squares = squares + jnp.sum(wide * wide, axis=-1, keepdims=True)
+    scale = lax.rsqrt(squares / hidden_ref.shape[1] + epsilon)
+    for half in range(2):
+        wide = hidden_ref[:, cols[half]].astype(jnp.float32)
+        normed_ref[:, cols[half]] = (wide * scale * gain_ref[:, cols[half]]).astype(jnp.bfloat16)
+
+
+def ring_scatter(lhs, rhs, n, collective_id, finish=finish_plain, extras=(), outputs=1):
     m, reach = n // 2, n // 4
-    rows, width = x.shape[1:]
+    rows, width = lhs.shape[1] // 2, rhs.shape[1]
     piece = (2, reach, 2, rows, width // 2)
     return pl.pallas_call(
-        functools.partial(scatter_kernel, n),
-        out_shape=jax.ShapeDtypeStruct((rows, width), jnp.float32),
-        in_specs=[VMEM],
-        out_specs=VMEM,
+        functools.partial(scatter_kernel, n, finish, len(extras)),
+        out_shape=[jax.ShapeDtypeStruct((rows, width), jnp.bfloat16)] * outputs,
+        in_specs=[VMEM] * (2 + len(extras)),
+        out_specs=[VMEM] * outputs,
         scratch_shapes=[
+            pltpu.VMEM((m, 2, rows, width), jnp.bfloat16),
             pltpu.VMEM((m, rows, width), jnp.bfloat16),
             pltpu.VMEM(piece, jnp.bfloat16),
             pltpu.VMEM(piece, jnp.bfloat16),
@@ -239,94 +272,94 @@
         ],
         compiler_params=pltpu.CompilerParams(collective_id=collective_id, has_side_effects=True),
         name=f"scatter{collective_id}",
-    )(x)
-
-
-def exchange_kernel(n, x_ref, out_ref, send, recv):
+    )(lhs, rhs, *extras)
+
+
+def attend_kernel(n, key_count, q_ref, fresh_ref, cached_ref, out_ref, stage, send, recv):
     me = lax.axis_index("ctx")
+    rows = q_ref.shape[0]
+    per = QUERY_HEADS // n
+    group = HEADS_STEP // per
+    steps = n // group
+    scale = HEAD_SIZE ** (-0.5)
     greet([(me + j) % n for j in range(1, n)])
-    copies = []
-    for j in range(1, n):
-        other = (me + j) % n
-        copy = remote(x_ref.at[other], out_ref.at[me], send.at[j], recv.at[j], other)
-        copy.start()
-        copies.append(copy)
-    out_ref[me] = x_ref[me]
+
+    def heads_of(u):
+        pair = u * HEADS_STEP // (QUERY_HEADS // KEY_VALUE_HEADS)
+        lanes = pl.ds(pl.multiple_of(pair * HEAD_SIZE, HEAD_SIZE), HEAD_SIZE)
+        keys = cached_ref[:, :key_count, lanes].reshape(-1, HEAD_SIZE)
+        values = cached_ref[:, key_count : 2 * key_count, lanes].reshape(-1, HEAD_SIZE)
+        fresh_key = fresh_ref[0, :, lanes].astype(jnp.float32)
+        fresh_value = fresh_ref[1, :, lanes].astype(jnp.float32)
+        width = HEADS_STEP * HEAD_SIZE
+        block = q_ref[:, pl.ds(pl.multiple_of(u * width, width), width)]
+        heads = [block[:, h * HEAD_SIZE : (h + 1) * HEAD_SIZE] for h in range(HEADS_STEP)]
+        scores = (
+            lax.dot_general(
+                jnp.concatenate(heads, axis=0),
+                keys,
+                (((1,), (1,)), ((), ())),
+                preferred_element_type=jnp.float32,
+            )
+            * scale
+        )
+        own = jnp.concatenate(
+            [jnp.sum(q.astype(jnp.float32) * fresh_key, axis=-1, keepdims=True) for q in heads],
+            axis=0,
+        )
+        own = own * scale
+        peak = jnp.maximum(own, jnp.max(scores, axis=-1, keepdims=True))
+        weights = jnp.exp(scores - peak)
+        own = jnp.exp(own - peak)
+        totals = jnp.sum(weights, axis=-1, keepdims=True) + own
+        mixed = jnp.dot(weights.astype(jnp.bfloat16), values, preferred_element_type=jnp.float32)
+        for h in range(HEADS_STEP):
+            part = slice(h * rows, (h + 1) * rows)
+            result = (mixed[part] + own[part] * fresh_value) / totals[part]
+            column = (h % per) * HEAD_SIZE
+            stage[u * group + h // per, :, column : column + HEAD_SIZE] = result.astype(
+                jnp.bfloat16
+            )
+
+    def copy_to(other):
+        return remote(stage.at[other], out_ref.at[me], send.at[other], recv.at[me], other)
+
+    @pl.loop(0, steps - 1)
+    def _(s):
+        u = (me // group + 1 + s) % steps
+        heads_of(u)
+        for j in range(group):
+            copy_to(u * group + j).start()
+
+    heads_of(me // group)
+    near = [me // group * group + (me % group + j) % group for j in range(1, group)]
+    for other in near:
+        copy_to(other).start()
+    out_ref[me] = stage[me]
     for j in range(1, n):
         source = (me + n - j) % n
         piece = out_ref.at[source]
-        remote(piece, piece, send.at[j], recv.at[j], source).wait_recv()
-    for copy in copies:
-        copy.wait_send()
-
-
-def exchange(x, n, collective_id):
+        remote(piece, piece, send.at[source], recv.at[source], source).wait_recv()
+    for j in range(1, n):
+        copy_to((me + j) % n).wait_send()
+
+
+def attend(queries, fresh_key_value, gathered, key_count, n, collective_id):
+    rows = queries.shape[0]
+    shape = (n, rows, QUERY_HEADS // n * HEAD_SIZE)
     return pl.pallas_call(
-        functools.partial(exchange_kernel, n),
-        out_shape=jax.ShapeDtypeStruct(x.shape, x.dtype),
-        in_specs=[VMEM],
+        functools.partial(attend_kernel, n, key_count),
+        out_shape=jax.ShapeDtypeStruct(shape, jnp.bfloat16),
+        in_specs=[VMEM] * 3,
         out_specs=VMEM,
-        scratch_shapes=[pltpu.SemaphoreType.DMA((n,)), pltpu.SemaphoreType.DMA((n,))],
+        scratch_shapes=[
+            pltpu.VMEM(shape, jnp.bfloat16),
+            pltpu.SemaphoreType.DMA((n,)),
+            pltpu.SemaphoreType.DMA((n,)),
+        ],
         compiler_params=pltpu.CompilerParams(collective_id=collective_id, has_side_effects=True),
-        name=f"exchange{collective_id}",
-    )(x)
-
-
-def attend_kernel(per, q_ref, fresh_key_ref, fresh_value_ref, key_ref, value_ref, out_ref):
-    rows = q_ref.shape[0]
-    keys = key_ref[...].reshape(-1, HEAD_SIZE)
-    values = value_ref[...].reshape(-1, HEAD_SIZE)
-    fresh_key = fresh_key_ref[...].astype(jnp.float32)
-    fresh_value = fresh_value_ref[...].astype(jnp.float32)
-    scale = HEAD_SIZE ** (-0.5)
-    heads = [q_ref[:, h * HEAD_SIZE : (h + 1) * HEAD_SIZE] for h in range(HEADS_STEP)]
-    scores = (
-        lax.dot_general(
-            jnp.concatenate(heads, axis=0),
-            keys,
-            (((1,), (1,)), ((), ())),
-            preferred_element_type=jnp.float32,
-        )
-        * scale
-    )
-    own = jnp.concatenate(
-        [jnp.sum(q.astype(jnp.float32) * fresh_key, axis=-1, keepdims=True) for q in heads], axis=0
-    )
-    own = own * scale
-    peak = jnp.maximum(own, jnp.max(scores, axis=-1, keepdims=True))
-    weights = jnp.exp(scores - peak)
-    own = jnp.exp(own - peak)
-    totals = jnp.sum(weights, axis=-1, keepdims=True) + own
-    mixed = jnp.dot(weights.astype(jnp.bfloat16), values, preferred_element_type=jnp.float32)
-    for h in range(HEADS_STEP):
-        part = slice(h * rows, (h + 1) * rows)
-        result = (mixed[part] + own[part] * fresh_value) / totals[part]
-        column = (h % per) * HEAD_SIZE
-        out_ref[h // per, :, column : column + HEAD_SIZE] = result.astype(jnp.bfloat16)
-
-
-def attend(queries, fresh_key_value, gathered, key_count, n):
-    rows = queries.shape[0]
-    per = QUERY_HEADS // n
-    parts = QUERY_HEADS // KEY_VALUE_HEADS // HEADS_STEP
-    fresh = lambda i: pl.BlockSpec((None, rows, HEAD_SIZE), lambda g, s, i=i: (i, 0, g))
-    cached = lambda i: pl.BlockSpec((n, key_count, HEAD_SIZE), lambda g, s, i=i: (0, i, g))
-    return pl.pallas_call(
-        functools.partial(attend_kernel, per),
-        grid=(KEY_VALUE_HEADS, parts),
-        out_shape=jax.ShapeDtypeStruct((n, rows, per * HEAD_SIZE), jnp.bfloat16),
-        in_specs=[
-            pl.BlockSpec((rows, HEADS_STEP * HEAD_SIZE), lambda g, s: (0, g * parts + s)),
-            fresh(0),
-            fresh(1),
-            cached(0),
-            cached(1),
-        ],
-        out_specs=pl.BlockSpec(
-            (HEADS_STEP // per, rows, per * HEAD_SIZE), lambda g, s: (g * parts + s, 0, 0)
-        ),
         name="attend",
-    )(queries, fresh_key_value, fresh_key_value, gathered, gathered)
+    )(queries, fresh_key_value, gathered)
 
 
 def local(
@@ -379,22 +412,20 @@
     ranks = jnp.where(named, ranks, -1)
     chosen = ranks[:, None, :] == jnp.arange(capacity)[None, :, None]
     pick = chosen.astype(jnp.bfloat16).reshape(local_count * capacity, n * rows)
-    spread = jnp.where(chosen, my_shares[:, None, :], jnp.zeros((), jnp.bfloat16)).reshape(
-        local_count * capacity, n * rows
-    )
-
-    attention = exchange(attend(queries, fresh_key_value, gathered, key_count, n), n, 1)
-    projected = jnp.dot(
-        attention.reshape(n * rows, -1), out_proj, preferred_element_type=jnp.float32
-    ).astype(jnp.bfloat16)
-    projected = ring_scatter(projected.reshape(n, rows, D), n, 2)
-    hidden = (residual.astype(jnp.float32) + projected).astype(jnp.bfloat16)
-    hidden_wide = hidden.astype(jnp.float32)
-    normed = (
-        hidden_wide
-        * lax.rsqrt(jnp.mean(hidden_wide * hidden_wide, axis=-1, keepdims=True) + epsilon)
-        * norm_gain
-    ).astype(jnp.bfloat16)
+    spread = jnp.where(
+        ranks.T[:, :, None] == jnp.arange(capacity), my_shares.T[:, :, None], jnp.zeros((), jnp.bfloat16)
+    ).reshape(n * rows, local_count * capacity)
+
+    attention = attend(queries, fresh_key_value, gathered, key_count, n, 1)
+    hidden, normed = ring_scatter(
+        attention.reshape(n // 2, 2 * rows, -1),
+        out_proj,
+        n,
+        2,
+        finish_normed,
+        (residual, norm_gain.reshape(1, D)),
+        2,
+    )
     all_normed = ring_gather(normed, n, 3).reshape(n * rows, D)
 
     inputs = (
@@ -407,13 +438,9 @@
     produced = jnp.einsum(
         "emf,efd->emd", active, w_down, preferred_element_type=jnp.float32
     ).astype(jnp.bfloat16)
-    combined = lax.dot_general(
-        spread,
-        produced.reshape(local_count * capacity, D),
-        (((0,), (0,)), ((), ())),
-        preferred_element_type=jnp.float32,
-    ).astype(jnp.bfloat16)
-    expert_out = ring_scatter(combined.reshape(n, rows, D), n, 4).astype(jnp.bfloat16)
+    (expert_out,) = ring_scatter(
+        spread.reshape(n // 2, 2 * rows, -1), produced.reshape(local_count * capacity, D), n, 4
+    )
     return (hidden, expert_out)
 
 

time: 217 us -> 216 us (level)
  local copies, waits for them, and re-layouts: 1.62 us -> 22.3 us
  matrix products: 36.9 us -> 22.3 us
  Pallas kernels: 164 us -> 157 us
    eq x0 -> x4, local copies, waits for them, and re-layouts: none -> 13.2 us  [local(): ranks.T[:, :, None] == jnp.arange(capacity)]
    dot_general x2 -> x1, matrix products: 18 us -> 4.89 us  [local(): jnp.einsum('emf,efd->emd', active, w_down, preferred_element_type=jnp.flo...]
    pallas_call x4 -> x3, Pallas kernels: 100 us -> 93.1 us  [the longest x2 67.9 us: ring_scatter(): pl.pallas_call(functools.partial(scatter_kernel, n, finish, len(extras)),...]
    broadcast_in_dim x0 -> x2, local copies, waits for them, and re-layouts: none -> 5.57 us  [local(): jnp.where(ranks.T[:, :, None] == jnp.arange(capacity), my_shares.T[:, :,...]
    select_n x0 -> x1, other arithmetic: none -> 4.59 us  [local(): jnp.where(ranks.T[:, :, None] == jnp.arange(capacity), my_shares.T[:, :,...]
    convert_element_type x2 -> x0, other arithmetic: 2.72 us -> none  [the longest x1 1.85 us: local(): ring_scatter(combined.reshape(n, rows, D), n, 4).astype(jnp.bfloat16)]
    unnamed x10 -> x11, local copies, waits for them, and re-layouts: 0.03 us -> 2.7 us
where the time goes in v2:
time: 216 us; the launch traced here: 213 us
  Pallas kernels  157 us (73%)
  local copies, waits for them, and re-layouts  22.3 us (10%)
  matrix products  22.3 us (10%)
  other arithmetic  10.5 us (5%)
    pallas_call x2, Pallas kernels, ring_scatter(): pl.pallas_call(functools.partial(scatter_kernel, n, finish, len(extras)),...  67.9 us
    pallas_call x2, Pallas kernels, ring_gather(): pl.pallas_call(functools.partial(gather_kernel, n), out_shape=jax.ShapeDt...  64 us
    pallas_call x1, Pallas kernels, attend(): pl.pallas_call(functools.partial(attend_kernel, n, key_count), out_shape=...  25.2 us
    eq x4, local copies, waits for them, and re-layouts, local(): ranks.T[:, :, None] == jnp.arange(capacity)  13.2 us
    dot_general x1, matrix products, local(): jnp.einsum('emd,edf->emf', inputs, w_gate_up, preferred_element_type=jnp....  9.11 us
    dot_general x1, matrix products, local(): jnp.dot(pick, all_normed, preferred_element_type=jnp.float32)  8.27 us
    broadcast_in_dim x2, local copies, waits for them, and re-layouts, local(): jnp.where(ranks.T[:, :, None] == jnp.arange(capacity), my_shares.T[:, :,...  5.57 us
    dot_general x1, matrix products, local(): jnp.einsum('emf,efd->emd', active, w_down, preferred_element_type=jnp.flo...  4.89 us

profile of v2, /device:TPU:13, one launch (start us, length us, event | category | flops | bytes accessed | tf_op | source)
XLA Modules:
  0.0 212.9 jit_solution(3550400920912040599)
XLA Ops:
  0.6 0.7 reduce_sum.28
  1.3 0.7 broadcast_divide_fusion
  2.0 0.1 copy.29
  2.1 0.8 select_reduce_fusion.1
  2.9 0.1 copy.28
  3.0 0.3 select_reduce_fusion
  3.3 1.7 fusion.4.x_ref
  5.0 31.2 %gather0.1.cached_ref = bf16[16,288,512]{2,1,0:T(8,128)(2,1)} custom-call(bf16[288,512]{1,0:T(8,128)(2,1)} %fusion.4.x_ref), custom_call_target="tpu_custom_call" | custom-call | tf_op jit(solution)/shard_map/gather0/pallas_call | solution.py:129
  36.2 0.0 slice-start
  36.2 25.2 %attend.1 = bf16[16,80,256]{2,1,0:T(8,128)(2,1)} custom-call(bf16[80,4096]{1,0:T(8,128)(2,1)} %q_ref.1, bf16[2,80,512]{2,1,0:T(8,128)(2,1)} %fresh_ref.1, bf16[16,288,512]{2,1,0:T(8,128)(2,1)} %gather0.1.cached_ref), custom_call_target="tpu_custom_call" | custom-call | tf_op jit(solution)/shard_map/attend/pallas_call | solution.py:350
  61.4 32.6 %scatter2.1 = (bf16[80,2048]{1,0:T(8,128)(2,1)}, bf16[80,2048]{1,0:T(8,128)(2,1)}) custom-call(bf16[8,160,256]{2,1,0:T(8,128)(2,1)} %bitcast.23, bf16[256,2048]{1,0:T(8,128)(2,1)} %rhs_ref.1, bf16[80,2048]{1,0:T(8,128)(2,1)} %refs_0_.1, f32[1,2048]{1,0:T(1,128)} %bitcast.27), custom_call_target="tpu_custom_call" | custom-call | tf_op jit(solution)/shard_map/scatter2/pallas_call | solution.py:258
  94.0 0.0 slice-done
  94.0 0.2 reshape.87
  94.2 0.2 broadcast_compare_fusion
  94.5 1.8 broadcast_in_dim.51
  96.2 3.8 %broadcast_in_dim.52 = bf16[8,160,960]{2,1,0:T(8,128)(2,1)} reshape(bf16[1280,2,480]{2,1,0:T(2,128)(2,1)S(1)} %broadcast_in_dim.51) | data formatting | bytes 4915200 | tf_op jit(solution)/shard_map/jit(_where)/broadcast_in_dim | solution.py:415
  100.0 0.2 copy.35
  100.3 0.6 reduce-window.6
  100.9 0.2 slice_reduce_fusion
  101.1 0.2 reduce-window.9
  101.3 0.1 add_bitcast_fusion
  101.4 0.3 copy.31
  101.6 4.0 %eq.75 = s32[1280,2,480]{2,1,0:T(2,128)} broadcast(s32[1280,2]{1,0:T(8,128)S(1)} %copy.31), dimensions={0,1} | broadcast | bytes 4925440 | tf_op jit(solution)/shard_map/eq | solution.py:416
  105.6 0.0 copy-start
  105.6 9.1 %eq.76 = s32[8,160,960]{2,1,0:T(8,128)} reshape(s32[1280,2,480]{2,1,0:T(2,128)} %eq.75) | data formatting | bytes 9830400 | tf_op jit(solution)/shard_map/eq | solution.py:416
  114.7 0.1 eq.78
  114.8 0.0 copy-done
  114.8 4.6 %compare_select_fusion.lhs_ref = bf16[8,160,960]{2,1,0:T(8,128)(2,1)} fusion(bf16[8,160,960]{2,1,0:T(8,128)(2,1)S(1)} %copy-done, s32[8,160,960]{2,1,0:T(8,128)} %eq.76, s32[960]{0:T(1024)S(1)} %eq.78), kind=kLoop, calls=%fused_computation | loop fusion | flops 2457600 | bytes 9834240 | tf_op jit(solution)/shard_map/jit(_where)/select_n | solution.py:415
  119.4 0.7 iota_compare_fusion
  120.0 32.8 %gather3.1 = bf16[16,80,2048]{2,1,0:T(8,128)(2,1)} custom-call(bf16[80,2048]{1,0:T(8,128)(2,1)} %get-tuple-element.5.x_ref), custom_call_target="tpu_custom_call" | custom-call | tf_op jit(solution)/shard_map/gather3/pallas_call | solution.py:129
  152.8 0.0 slice-start.1
  152.9 8.3 %convolution_convert_fusion.1 = bf16[960,2048]{1,0:T(8,128)(2,1)S(1)} fusion(pred[960,1280]{1,0:T(32,128)(4,1)S(1)} %bitcast.24, bf16[1280,2048]{1,0:T(8,128)(2,1)} %bitcast.21), kind=kOutput, calls=%fused_computation.3 | convolution fusion | flops 5035130880 | bytes 10403840 | tf_op jit(solution)/shard_map/dot_general | solution.py:432
  161.1 0.0 slice-start.2
  161.1 9.1 %fusion.6 = f32[2,480,1536]{2,1,0:T(8,128)S(1)} fusion(bf16[2,480,2048]{2,1,0:T(8,128)(2,1)S(1)} %bitcast.31, bf16[2,2048,1536]{2,1,0:T(8,128)(2,1)} %param.17), kind=kOutput, calls=%fused_computation.22 | convolution fusion | flops 6039797760 | bytes 22413312 | tf_op jit(solution)/shard_map/emd,edf->emf/dot_general | solution.py:436
  170.3 0.0 slice-done.1
  170.3 0.0 slice-done.2
  170.3 4.9 %convolution_convert_fusion = bf16[2,480,2048]{2,1,0:T(8,128)(2,1)} fusion(bf16[2,768,2048]{2,1,0:T(8,128)(2,1)S(1)} %bitcast.30, f32[2,480,1536]{2,1,0:T(8,128)S(1)} %fusion.6), kind=kOutput, calls=%fused_computation.2 | convolution fusion | flops 3026288640 | bytes 16121856 | tf_op jit(solution)/shard_map/emf,efd->emd/dot_general | solution.py:438
  175.2 0.0 copy-start.1
  175.2 35.3 %scatter4.1 = bf16[80,2048]{1,0:T(8,128)(2,1)} custom-call(bf16[8,160,960]{2,1,0:T(8,128)(2,1)} %compare_select_fusion.lhs_ref, bf16[960,2048]{1,0:T(8,128)(2,1)} %bitcast.22), custom_call_target="tpu_custom_call" | custom-call | tf_op jit(solution)/shard_map/scatter4/pallas_call | solution.py:258
  210.5 0.0 copy-done.1
  210.5 0.7 copy.41
  211.2 1.7 copy.42
  (6 shorter events, 0.1 us)
Async XLA Ops:
  36.2 57.8 %slice-start = ((bf16[16,288,512]{2,1,0:T(8,128)(2,1)}), bf16[16,20,512]{2,1,0:T(8,128)(2,1)S(1)}, s32[]{:S(2)}) async-start(bf16[16,288,512]{2,1,0:T(8,128)(2,1)} %gather0.1.cached_ref), calls=%async_computation | async-start | bytes 786432 | tf_op jit(solution)/shard_map/slice | solution.py:406
  105.6 9.2 %copy-start = (bf16[8,160,960]{2,1,0:T(8,128)(2,1)S(1)}, bf16[8,160,960]{2,1,0:T(8,128)(2,1)}, u32[]{:S(2)}) copy-start(bf16[8,160,960]{2,1,0:T(8,128)(2,1)} %broadcast_in_dim.52) | copy-start | bytes 7372804
  152.8 17.4 %slice-start.1 = ((s8[6291456]{0:T(1024)(128)(4,1)}), s8[4194304]{0:T(1024)(128)(4,1)S(1)}, s32[]{:S(2)}) async-start(s8[6291456]{0:T(1024)(128)(4,1)} %bitcast.29), calls=%async_computation.1 | async-start | bytes 8388608
  161.1 9.1 %slice-start.2 = ((s8[6291456]{0:T(1024)(128)(4,1)}), s8[2097152]{0:T(1024)(128)(4,1)S(1)}, s32[]{:S(2)}) async-start(s8[6291456]{0:T(1024)(128)(4,1)} %bitcast.29), calls=%async_computation.2 | async-start | bytes 4194304
  175.2 35.3 %copy-start.1 = (bf16[80,2048]{1,0:T(8,128)(2,1)S(1)}, bf16[80,2048]{1,0:T(8,128)(2,1)}, u32[]{:S(2)}) copy-start(bf16[80,2048]{1,0:T(8,128)(2,1)} %get-tuple-element.10) | copy-start | bytes 983044

commit v3 on v2

--- a/solution.py
+++ b/solution.py
@@ -67,7 +67,7 @@
 PAIRS = ((RIGHT, 0), (LEFT, 1), (RIGHT, 1), (LEFT, 0))
 
 
-def gather_kernel(n, x_ref, out_ref, ring_send, ring_recv, mate_send, mate_recv):
+def gather_kernel(n, x_ref, out_ref, ring_send, ring_recv, mate_send, mate_recv, work=None):
     m, reach = n // 2, n // 4
     me, core, at = ring(m)
     mate = at(0, 1 - core)
@@ -94,7 +94,41 @@
     copy.start()
     started.append(copy)
     out_ref[me] = x_ref[...]
+    def wait_mate(offset):
+        if offset == 0:
+            theirs = out_ref.at[mate]
+            remote(theirs, theirs, mate_send.at[0, 0, 0], mate_recv.at[0, 0, 0], mate).wait_recv()
+            return
+        d = abs(offset)
+        for way, half in PAIRS:
+            if travels(way, half, d, reach) and (d == reach or (way == RIGHT) == (offset < 0)):
+                piece = out_ref.at[at(offset, 1 - core), :, cols[half]]
+                remote(
+                    piece, piece, mate_send.at[way, d, half], mate_recv.at[way, d, half], mate
+                ).wait_recv()
+
+    def offsets_at(d):
+        return [d] if d in (0, reach) else [-d, d]
+
+    def jobs_at(d):
+        jobs = []
+        for offset in offsets_at(d):
+            chip = at(offset, 0) // 2
+
+            def first(offset=offset, chip=chip):
+                wait_mate(offset)
+                if work is not None:
+                    work(chip, 0, offset == 0)
+
+            def second(offset=offset, chip=chip):
+                if work is not None:
+                    work(chip, 1, offset == 0)
+
+            jobs += [first, second]
+        return jobs
+
     for d in range(1, reach + 1):
+        jobs = jobs_at(d - 1)
         for way, half in PAIRS:
             if not travels(way, half, d, reach):
                 continue
@@ -110,18 +144,61 @@
             )
             copy.start()
             started.append(copy)
-    theirs = out_ref.at[mate]
-    remote(theirs, theirs, mate_send.at[0, 0, 0], mate_recv.at[0, 0, 0], mate).wait_recv()
-    for d in range(1, reach + 1):
-        for way, half in PAIRS:
-            if travels(way, half, d, reach):
-                owner = at(-d if way == RIGHT else d, 1 - core)
-                piece = out_ref.at[owner, :, cols[half]]
-                remote(
-                    piece, piece, mate_send.at[way, d, half], mate_recv.at[way, d, half], mate
-                ).wait_recv()
+            if jobs:
+                jobs.pop(0)()
+        for job in jobs:
+            job()
+    for job in jobs_at(reach):
+        job()
     for copy in started:
         copy.wait_send()
+
+
+def pick_kernel(n, x_ref, place_ref, out_ref, held, chosen, *semaphores):
+    count = place_ref.shape[1]
+    rows, width = x_ref.shape
+    depth = out_ref.shape[0]
+
+    def work(chip, half, start):
+        if half == 0:
+            places = lax.broadcasted_iota(jnp.int32, (depth, 2 * rows), 0).astype(jnp.float32)
+            marks = jnp.zeros((depth, 2 * rows), jnp.float32)
+            table = place_ref[chip]
+            for e in range(count):
+                marks = jnp.where(places == table[e : e + 1], 1.0, marks)
+            chosen[...] = marks.astype(jnp.bfloat16)
+        steps = width // 2 // COLUMNS_STEP
+
+        @pl.loop(half * steps, (half + 1) * steps)
+        def _(c):
+            part = pl.ds(pl.multiple_of(c * COLUMNS_STEP, COLUMNS_STEP), COLUMNS_STEP)
+            block = held[pl.ds(chip * 2, 2), :, part].reshape(2 * rows, COLUMNS_STEP)
+            picked = jnp.dot(chosen[...], block, preferred_element_type=jnp.float32)
+            picked = picked.astype(jnp.bfloat16)
+            out_ref[:, part] = picked if start else out_ref[:, part] + picked
+
+    gather_kernel(n, x_ref, held, *semaphores, work=work)
+
+
+def ring_pick(x, places, depth, n, collective_id):
+    reach = n // 4
+    rows, width = x.shape
+    return pl.pallas_call(
+        functools.partial(pick_kernel, n),
+        out_shape=jax.ShapeDtypeStruct((depth, width), x.dtype),
+        in_specs=[VMEM] * 2,
+        out_specs=VMEM,
+        scratch_shapes=[
+            pltpu.VMEM((n, rows, width), x.dtype),
+            pltpu.VMEM((depth, 2 * rows), x.dtype),
+            pltpu.SemaphoreType.DMA((2, reach, 2)),
+            pltpu.SemaphoreType.DMA((2, reach, 2)),
+            pltpu.SemaphoreType.DMA((2, reach + 1, 2)),
+            pltpu.SemaphoreType.DMA((2, reach + 1, 2)),
+        ],
+        compiler_params=pltpu.CompilerParams(collective_id=collective_id, has_side_effects=True),
+        name=f"pick{collective_id}",
+    )(x, places)
 
 
 def ring_gather(x, n, collective_id):
@@ -142,7 +219,7 @@
     )(x)
 
 
-def scatter_kernel(n, finish, extras, lhs_ref, rhs_ref, *refs):
+def scatter_kernel(n, finish, left, extras, lhs_ref, rhs_ref, *refs):
     extra_refs, refs = refs[:extras], refs[extras:]
     outs, scratch = refs[:-8], refs[-8:]
     made, from_mate, outgoing, incoming, ring_send, ring_recv, mate_send, mate_recv = scratch
@@ -163,12 +240,12 @@
 
     def make(offset):
         k = offsets.index(offset)
-        lhs = lhs_ref.at[at(offset, 0) // 2]
+        lhs = left(lhs_ref[at(offset, 0) // 2], rhs_ref.shape[0])
 
         @pl.loop(0, width // COLUMNS_STEP)
         def _(c):
             part = pl.ds(pl.multiple_of(c * COLUMNS_STEP, COLUMNS_STEP), COLUMNS_STEP)
-            product = jnp.dot(lhs[...], rhs_ref[:, part], preferred_element_type=jnp.float32)
+            product = jnp.dot(lhs, rhs_ref[:, part], preferred_element_type=jnp.float32)
             product = product.astype(jnp.bfloat16)
             made[k, 0, :, part] = product[:rows]
             made[k, 1, :, part] = product[rows:]
@@ -251,12 +328,29 @@
         normed_ref[:, cols[half]] = (wide * scale * gain_ref[:, cols[half]]).astype(jnp.bfloat16)
 
 
-def ring_scatter(lhs, rhs, n, collective_id, finish=finish_plain, extras=(), outputs=1):
+def as_it_is(lhs, depth):
+    return lhs
+
+
+def spread(lhs, depth):
+    count = lhs.shape[1] // 2
+    places = lax.broadcasted_iota(jnp.int32, (lhs.shape[0], depth), 1).astype(jnp.float32)
+    total = jnp.zeros((lhs.shape[0], depth), jnp.float32)
+    for e in range(count):
+        total = jnp.where(
+            places == lhs[:, e : e + 1], lhs[:, count + e : count + e + 1], total
+        )
+    return total.astype(jnp.bfloat16)
+
+
+def ring_scatter(
+    lhs, rhs, n, collective_id, left=as_it_is, finish=finish_plain, extras=(), outputs=1
+):
     m, reach = n // 2, n // 4
     rows, width = lhs.shape[1] // 2, rhs.shape[1]
     piece = (2, reach, 2, rows, width // 2)
     return pl.pallas_call(
-        functools.partial(scatter_kernel, n, finish, len(extras)),
+        functools.partial(scatter_kernel, n, finish, left, len(extras)),
         out_shape=[jax.ShapeDtypeStruct((rows, width), jnp.bfloat16)] * outputs,
         in_specs=[VMEM] * (2 + len(extras)),
         out_specs=[VMEM] * outputs,
@@ -409,12 +503,11 @@
     my_shares = lax.dynamic_slice(all_shares, (0, mine), (n * rows, local_count)).T
     named = my_shares > 0
     ranks = jnp.cumsum(named.astype(jnp.int32), axis=1) - 1
-    ranks = jnp.where(named, ranks, -1)
-    chosen = ranks[:, None, :] == jnp.arange(capacity)[None, :, None]
-    pick = chosen.astype(jnp.bfloat16).reshape(local_count * capacity, n * rows)
-    spread = jnp.where(
-        ranks.T[:, :, None] == jnp.arange(capacity), my_shares.T[:, :, None], jnp.zeros((), jnp.bfloat16)
-    ).reshape(n * rows, local_count * capacity)
+    starts = jnp.arange(local_count)[:, None] * capacity
+    places = jnp.where(named, ranks + starts, -1).astype(jnp.float32)
+    table = places.reshape(local_count, n // 2, 2 * rows).transpose(1, 0, 2)
+    listed = jnp.concatenate([places, my_shares.astype(jnp.float32)], axis=0)
+    listed = listed.reshape(2 * local_count, n // 2, 2 * rows).transpose(1, 2, 0)
 
     attention = attend(queries, fresh_key_value, gathered, key_count, n, 1)
     hidden, normed = ring_scatter(
@@ -422,24 +515,20 @@
         out_proj,
         n,
         2,
+        as_it_is,
         finish_normed,
         (residual, norm_gain.reshape(1, D)),
         2,
     )
-    all_normed = ring_gather(normed, n, 3).reshape(n * rows, D)
-
-    inputs = (
-        jnp.dot(pick, all_normed, preferred_element_type=jnp.float32)
-        .astype(jnp.bfloat16)
-        .reshape(local_count, capacity, D)
-    )
+    inputs = ring_pick(normed, table, local_count * capacity, n, 3)
+    inputs = inputs.reshape(local_count, capacity, D)
     both = jnp.einsum("emd,edf->emf", inputs, w_gate_up, preferred_element_type=jnp.float32)
     active = (jax.nn.silu(both[..., :FF]) * both[..., FF:]).astype(jnp.bfloat16)
     produced = jnp.einsum(
         "emf,efd->emd", active, w_down, preferred_element_type=jnp.float32
     ).astype(jnp.bfloat16)
     (expert_out,) = ring_scatter(
-        spread.reshape(n // 2, 2 * rows, -1), produced.reshape(local_count * capacity, D), n, 4
+        listed, produced.reshape(local_count * capacity, D), n, 4, spread
     )
     return (hidden, expert_out)
 

time: 216 us -> 190 us (0.88)
  local copies, waits for them, and re-layouts: 22.3 us -> 5.21 us
  matrix products: 22.3 us -> 15 us
  other arithmetic: 10.5 us -> 5.1 us
  Pallas kernels: 157 us -> 160 us
    pallas_call x2 -> x3, Pallas kernels: 67.9 us -> 104 us  [the longest x2 68.3 us: ring_scatter(): pl.pallas_call(functools.partial(scatter_kernel, n, finish, left, len(ext...]
    pallas_call x2 -> x1, Pallas kernels: 64 us -> 31.3 us  [ring_gather(): pl.pallas_call(functools.partial(gather_kernel, n), out_shape=jax.ShapeDt...]
    eq x4 -> x0, local copies, waits for them, and re-layouts: 13.2 us -> none  [local(): ranks.T[:, :, None] == jnp.arange(capacity)]
    dot_general x1 -> x0, matrix products: 8.27 us -> none  [local(): jnp.dot(pick, all_normed, preferred_element_type=jnp.float32)]
    broadcast_in_dim x2 -> x0, local copies, waits for them, and re-layouts: 5.57 us -> none  [local(): jnp.where(ranks.T[:, :, None] == jnp.arange(capacity), my_shares.T[:, :,...]
    select_n x2 -> x0, other arithmetic: 4.61 us -> none  [the longest x1 4.59 us: local(): jnp.where(ranks.T[:, :, None] == jnp.arange(capacity), my_shares.T[:, :,...]
where the time goes in v3:
time: 190 us; the launch traced here: 187 us
  Pallas kernels  160 us (84%)
  matrix products  15 us (8%)
  local copies, waits for them, and re-layouts  5.21 us (3%)
  other arithmetic  5.1 us (3%)
    pallas_call x2, Pallas kernels, ring_scatter(): pl.pallas_call(functools.partial(scatter_kernel, n, finish, left, len(ext...  68.3 us
    pallas_call x1, Pallas kernels, ring_pick(): pl.pallas_call(functools.partial(pick_kernel, n), out_shape=jax.ShapeDtyp...  35.7 us
    pallas_call x1, Pallas kernels, ring_gather(): pl.pallas_call(functools.partial(gather_kernel, n), out_shape=jax.ShapeDt...  31.3 us
    pallas_call x1, Pallas kernels, attend(): pl.pallas_call(functools.partial(attend_kernel, n, key_count), out_shape=...  25.2 us
    dot_general x1, matrix products, local(): jnp.einsum('emd,edf->emf', inputs, w_gate_up, preferred_element_type=jnp....  10.1 us
    dot_general x1, matrix products, local(): jnp.einsum('emf,efd->emd', active, w_down, preferred_element_type=jnp.flo...  4.87 us

profile of v3, /device:TPU:13, one launch (start us, length us, event | category | flops | bytes accessed | tf_op | source)
XLA Modules:
  0.0 186.5 jit_solution(7366535620158909045)
XLA Ops:
  0.6 0.7 reduce_sum.28
  1.3 0.7 broadcast_divide_fusion
  2.0 0.8 select_reduce_fusion.1
  2.8 0.1 copy.38
  2.9 0.1 copy.39
  3.0 0.3 select_reduce_fusion
  3.3 1.7 fusion.4.x_ref
  5.0 31.3 %gather0.1.cached_ref = bf16[16,288,512]{2,1,0:T(8,128)(2,1)} custom-call(bf16[288,512]{1,0:T(8,128)(2,1)} %fusion.4.x_ref), custom_call_target="tpu_custom_call" | custom-call | tf_op jit(solution)/shard_map/gather0/pallas_call | solution.py:206
  36.3 0.0 slice-start
  36.3 25.2 %attend.1 = bf16[16,80,256]{2,1,0:T(8,128)(2,1)} custom-call(bf16[80,4096]{1,0:T(8,128)(2,1)} %q_ref.1, bf16[2,80,512]{2,1,0:T(8,128)(2,1)} %fresh_ref.1, bf16[16,288,512]{2,1,0:T(8,128)(2,1)} %gather0.1.cached_ref), custom_call_target="tpu_custom_call" | custom-call | tf_op jit(solution)/shard_map/attend/pallas_call | solution.py:444
  61.5 0.0 slice-done
  61.5 0.2 reshape.56
  61.7 0.2 constant_dynamic-slice_fusion
  61.8 0.2 copy.43
  62.0 32.6 %scatter2.1 = (bf16[80,2048]{1,0:T(8,128)(2,1)}, bf16[80,2048]{1,0:T(8,128)(2,1)}) custom-call(bf16[8,160,256]{2,1,0:T(8,128)(2,1)} %bitcast.30, bf16[256,2048]{1,0:T(8,128)(2,1)} %rhs_ref.1, bf16[80,2048]{1,0:T(8,128)(2,1)} %refs_0_.1, f32[1,2048]{1,0:T(1,128)} %bitcast.34), custom_call_target="tpu_custom_call" | custom-call | tf_op jit(solution)/shard_map/scatter2/pallas_call | solution.py:352
  94.6 0.6 reduce-window.6
  95.2 0.2 slice_reduce_fusion
  95.4 0.2 reduce-window.9
  95.6 0.1 add_bitcast_fusion
  95.7 0.1 fusion.5
  95.8 0.1 reshape.60
  95.8 0.6 copy.47
  96.5 1.1 copy.41
  97.6 0.0 slice-start.1
  97.6 35.7 %pick3.1 = bf16[960,2048]{1,0:T(8,128)(2,1)} custom-call(bf16[80,2048]{1,0:T(8,128)(2,1)} %get-tuple-element.5.x_ref, f32[8,2,160]{2,1,0:T(2,128)} %bitcast.33), custom_call_target="tpu_custom_call" | custom-call | tf_op jit(solution)/shard_map/pick3/pallas_call | solution.py:186
  133.3 0.0 slice-start.2
  133.3 10.1 %fusion.7 = f32[2,480,1536]{2,1,0:T(8,128)S(1)} fusion(bf16[2,480,2048]{2,1,0:T(8,128)(2,1)} %bitcast.29, bf16[2,2048,1536]{2,1,0:T(8,128)(2,1)} %param.17), kind=kOutput, calls=%fused_computation.24 | convolution fusion | flops 6039797760 | bytes 22413312 | tf_op jit(solution)/shard_map/emd,edf->emf/dot_general | solution.py:525
  143.5 0.0 slice-done.1
  143.5 0.0 slice-done.2
  143.5 4.9 %convolution_convert_fusion = bf16[2,480,2048]{2,1,0:T(8,128)(2,1)} fusion(bf16[2,768,2048]{2,1,0:T(8,128)(2,1)S(1)} %bitcast.37, f32[2,480,1536]{2,1,0:T(8,128)S(1)} %fusion.7), kind=kOutput, calls=%fused_computation | convolution fusion | flops 3026288640 | bytes 16121856 | tf_op jit(solution)/shard_map/emf,efd->emd/dot_general | solution.py:527
  148.4 0.0 copy-start
  148.4 35.7 %scatter4.1 = bf16[80,2048]{1,0:T(8,128)(2,1)} custom-call(f32[8,160,4]{2,1,0:T(8,128)} %bitcast.31, bf16[960,2048]{1,0:T(8,128)(2,1)} %bitcast.28), custom_call_target="tpu_custom_call" | custom-call | tf_op jit(solution)/shard_map/scatter4/pallas_call | solution.py:352
  184.1 0.0 copy-done
  184.1 0.7 copy.50
  184.8 1.7 copy.51
  (7 shorter events, 0.1 us)
Async XLA Ops:
  36.3 25.2 %slice-start = ((bf16[16,288,512]{2,1,0:T(8,128)(2,1)}), bf16[16,20,512]{2,1,0:T(8,128)(2,1)S(1)}, s32[]{:S(2)}) async-start(bf16[16,288,512]{2,1,0:T(8,128)(2,1)} %gather0.1.cached_ref), calls=%async_computation | async-start | bytes 786432 | tf_op jit(solution)/shard_map/slice | solution.py:500
  97.6 45.9 %slice-start.1 = ((s8[6291456]{0:T(1024)(128)(4,1)}), s8[2097152]{0:T(1024)(128)(4,1)S(1)}, s32[]{:S(2)}) async-start(s8[6291456]{0:T(1024)(128)(4,1)} %bitcast.36), calls=%async_computation.1 | async-start | bytes 4194304
  133.3 10.2 %slice-start.2 = ((s8[6291456]{0:T(1024)(128)(4,1)}), s8[4194304]{0:T(1024)(128)(4,1)S(1)}, s32[]{:S(2)}) async-start(s8[6291456]{0:T(1024)(128)(4,1)} %bitcast.36), calls=%async_computation.2 | async-start | bytes 8388608
  148.4 35.7 %copy-start = (bf16[80,2048]{1,0:T(8,128)(2,1)S(1)}, bf16[80,2048]{1,0:T(8,128)(2,1)}, u32[]{:S(2)}) copy-start(bf16[80,2048]{1,0:T(8,128)(2,1)} %get-tuple-element.8) | copy-start | bytes 983044

commit v4 on v3

--- a/solution.py
+++ b/solution.py
@@ -67,14 +67,15 @@
 PAIRS = ((RIGHT, 0), (LEFT, 1), (RIGHT, 1), (LEFT, 0))
 
 
-def gather_kernel(n, x_ref, out_ref, ring_send, ring_recv, mate_send, mate_recv, work=None):
+def gather_kernel(n, x_ref, out_ref, ring_send, ring_recv, mate_send, mate_recv, work=None, met=False):
     m, reach = n // 2, n // 4
     me, core, at = ring(m)
     mate = at(0, 1 - core)
     neighbour = (at(1, core), at(-1, core))
     half_width = x_ref.shape[1] // 2
     cols = [pl.ds(h * half_width, half_width) for h in range(2)]
-    greet((neighbour[0], neighbour[1], mate))
+    if not met:
+        greet((neighbour[0], neighbour[1], mate))
     started = []
 
     def forward(src, owner, way, half, d):
@@ -177,28 +178,7 @@
             picked = picked.astype(jnp.bfloat16)
             out_ref[:, part] = picked if start else out_ref[:, part] + picked
 
-    gather_kernel(n, x_ref, held, *semaphores, work=work)
-
-
-def ring_pick(x, places, depth, n, collective_id):
-    reach = n // 4
-    rows, width = x.shape
-    return pl.pallas_call(
-        functools.partial(pick_kernel, n),
-        out_shape=jax.ShapeDtypeStruct((depth, width), x.dtype),
-        in_specs=[VMEM] * 2,
-        out_specs=VMEM,
-        scratch_shapes=[
-            pltpu.VMEM((n, rows, width), x.dtype),
-            pltpu.VMEM((depth, 2 * rows), x.dtype),
-            pltpu.SemaphoreType.DMA((2, reach, 2)),
-            pltpu.SemaphoreType.DMA((2, reach, 2)),
-            pltpu.SemaphoreType.DMA((2, reach + 1, 2)),
-            pltpu.SemaphoreType.DMA((2, reach + 1, 2)),
-        ],
-        compiler_params=pltpu.CompilerParams(collective_id=collective_id, has_side_effects=True),
-        name=f"pick{collective_id}",
-    )(x, places)
+    gather_kernel(n, x_ref, held, *semaphores, work=work, met=True)
 
 
 def ring_gather(x, n, collective_id):
@@ -367,6 +347,60 @@
         compiler_params=pltpu.CompilerParams(collective_id=collective_id, has_side_effects=True),
         name=f"scatter{collective_id}",
     )(lhs, rhs, *extras)
+
+
+def scatter_pick_kernel(
+    n, lhs_ref, rhs_ref, residual_ref, gain_ref, place_ref, hidden_ref, out_ref, *scratch
+):
+    normed, scratch = scratch[0], scratch[1:]
+    scatter_kernel(
+        n,
+        finish_normed,
+        as_it_is,
+        2,
+        lhs_ref,
+        rhs_ref,
+        residual_ref,
+        gain_ref,
+        hidden_ref,
+        normed,
+        *scratch[:8],
+    )
+    pick_kernel(n, normed, place_ref, out_ref, *scratch[8:])
+
+
+def scatter_pick(lhs, rhs, residual, gain, places, depth, n, collective_id):
+    m, reach = n // 2, n // 4
+    rows, width = residual.shape
+    piece = (2, reach, 2, rows, width // 2)
+    return pl.pallas_call(
+        functools.partial(scatter_pick_kernel, n),
+        out_shape=[
+            jax.ShapeDtypeStruct((rows, width), jnp.bfloat16),
+            jax.ShapeDtypeStruct((depth, width), jnp.bfloat16),
+        ],
+        in_specs=[VMEM] * 5,
+        out_specs=[VMEM] * 2,
+        scratch_shapes=[
+            pltpu.VMEM((rows, width), jnp.bfloat16),
+            pltpu.VMEM((m, 2, rows, width), jnp.bfloat16),
+            pltpu.VMEM((m, rows, width), jnp.bfloat16),
+            pltpu.VMEM(piece, jnp.bfloat16),
+            pltpu.VMEM(piece, jnp.bfloat16),
+            pltpu.SemaphoreType.DMA((2, reach, 2)),
+            pltpu.SemaphoreType.DMA((2, reach, 2)),
+            pltpu.SemaphoreType.DMA((m,)),
+            pltpu.SemaphoreType.DMA((m,)),
+            pltpu.VMEM((n, rows, width), jnp.bfloat16),
+            pltpu.VMEM((depth, 2 * rows), jnp.bfloat16),
+            pltpu.SemaphoreType.DMA((2, reach, 2)),
+            pltpu.SemaphoreType.DMA((2, reach, 2)),
+            pltpu.SemaphoreType.DMA((2, reach + 1, 2)),
+            pltpu.SemaphoreType.DMA((2, reach + 1, 2)),
+        ],
+        compiler_params=pltpu.CompilerParams(collective_id=collective_id, has_side_effects=True),
+        name=f"scatter_pick{collective_id}",
+    )(lhs, rhs, residual, gain, places)
 
 
 def attend_kernel(n, key_count, q_ref, fresh_ref, cached_ref, out_ref, stage, send, recv):
@@ -481,7 +515,7 @@
     slots = jnp.sum(
         jnp.where(route_ids[..., None] == jnp.arange(expert_count), placement, 0), axis=-1
     )
-    slot_lanes = -(-expert_count // 128) * 128
+    slot_lanes = expert_count
     shares = jnp.sum(
         jnp.where(slots[..., None] == jnp.arange(slot_lanes), gate_share[..., None], 0.0), axis=1
     ).astype(jnp.bfloat16)
@@ -510,17 +544,16 @@
     listed = listed.reshape(2 * local_count, n // 2, 2 * rows).transpose(1, 2, 0)
 
     attention = attend(queries, fresh_key_value, gathered, key_count, n, 1)
-    hidden, normed = ring_scatter(
+    hidden, inputs = scatter_pick(
         attention.reshape(n // 2, 2 * rows, -1),
         out_proj,
+        residual,
+        norm_gain.reshape(1, D),
+        table,
+        local_count * capacity,
         n,
         2,
-        as_it_is,
-        finish_normed,
-        (residual, norm_gain.reshape(1, D)),
-        2,
-    )
-    inputs = ring_pick(normed, table, local_count * capacity, n, 3)
+    )
     inputs = inputs.reshape(local_count, capacity, D)
     both = jnp.einsum("emd,edf->emf", inputs, w_gate_up, preferred_element_type=jnp.float32)
     active = (jax.nn.silu(both[..., :FF]) * both[..., FF:]).astype(jnp.bfloat16)

time: 190 us -> 186 us (0.979)
  Pallas kernels: 160 us -> 157 us
    pallas_call x2 -> x1, Pallas kernels: 68.3 us -> 36.9 us  [ring_scatter(): pl.pallas_call(functools.partial(scatter_kernel, n, finish, left, len(ext...]
    pallas_call x1, Pallas kernels: 35.7 us -> 64.9 us  [scatter_pick(): pl.pallas_call(functools.partial(scatter_pick_kernel, n), out_shape=[jax....]
where the time goes in v4:
time: 186 us; the launch traced here: 183 us
  Pallas kernels  157 us (84%)
  matrix products  15 us (8%)
  local copies, waits for them, and re-layouts  5.19 us (3%)
  other arithmetic  4.88 us (3%)
    pallas_call x1, Pallas kernels, scatter_pick(): pl.pallas_call(functools.partial(scatter_pick_kernel, n), out_shape=[jax....  64.9 us
    pallas_call x1, Pallas kernels, ring_scatter(): pl.pallas_call(functools.partial(scatter_kernel, n, finish, left, len(ext...  36.9 us
    pallas_call x1, Pallas kernels, ring_gather(): pl.pallas_call(functools.partial(gather_kernel, n), out_shape=jax.ShapeDt...  29.8 us
    pallas_call x1, Pallas kernels, attend(): pl.pallas_call(functools.partial(attend_kernel, n, key_count), out_shape=...  25.1 us
    dot_general x1, matrix products, local(): jnp.einsum('emd,edf->emf', inputs, w_gate_up, preferred_element_type=jnp....  10.1 us
    dot_general x1, matrix products, local(): jnp.einsum('emf,efd->emd', active, w_down, preferred_element_type=jnp.flo...  4.83 us

profile of v4, /device:TPU:13, one launch (start us, length us, event | category | flops | bytes accessed | tf_op | source)
XLA Modules:
  0.0 182.6 jit_solution(1934598230042166554)
XLA Ops:
  0.6 0.7 reduce_sum.28
  1.3 0.7 broadcast_divide_fusion
  2.0 0.8 select_reduce_fusion.1
  2.9 0.1 copy.37
  3.0 0.1 convert_element_type.26
  3.1 1.7 fusion.4.x_ref
  4.8 29.8 %gather0.1.cached_ref = bf16[16,272,512]{2,1,0:T(8,128)(2,1)} custom-call(bf16[272,512]{1,0:T(8,128)(2,1)} %fusion.4.x_ref), custom_call_target="tpu_custom_call" | custom-call | tf_op jit(solution)/shard_map/gather0/pallas_call | solution.py:186
  34.6 0.0 slice-start
  34.6 25.1 %attend.1 = bf16[16,80,256]{2,1,0:T(8,128)(2,1)} custom-call(bf16[80,4096]{1,0:T(8,128)(2,1)} %q_ref.1, bf16[2,80,512]{2,1,0:T(8,128)(2,1)} %fresh_ref.1, bf16[16,272,512]{2,1,0:T(8,128)(2,1)} %gather0.1.cached_ref), custom_call_target="tpu_custom_call" | custom-call | tf_op jit(solution)/shard_map/attend/pallas_call | solution.py:478
  59.7 0.0 slice-done
  59.7 0.2 reshape.56
  60.0 0.2 constant_dynamic-slice_fusion
  60.1 0.2 copy.41
  60.3 0.6 reduce-window.6
  60.9 0.2 slice_reduce_fusion
  61.1 0.2 reduce-window.9
  61.3 0.1 add_bitcast_fusion
  61.4 0.1 fusion.5
  61.5 0.1 reshape.59
  61.5 0.6 copy.45
  62.2 1.1 copy.40
  63.3 0.0 slice-start.1
  63.3 64.9 %scatter_pick2.1 = (bf16[80,2048]{1,0:T(8,128)(2,1)}, bf16[960,2048]{1,0:T(8,128)(2,1)}) custom-call(bf16[8,160,256]{2,1,0:T(8,128)(2,1)} %bitcast.30, bf16[256,2048]{1,0:T(8,128)(2,1)} %rhs_ref.1, bf16[80,2048]{1,0:T(8,128)(2,1)} %residual_ref.1, f32[1,2048]{1,0:T(1,128)} %bitcast.33, f32[8,2,160]{2,1,0:T(2,128)} %bitcast.32), custom_call_target="tpu_custom_call" | custom-call | tf_op jit(solution)/shard_map/scatter_pick2/pallas_call | solution.py:376
  128.2 0.0 slice-start.2
  128.2 10.1 %fusion.7 = f32[2,480,1536]{2,1,0:T(8,128)S(1)} fusion(bf16[2,480,2048]{2,1,0:T(8,128)(2,1)} %bitcast.37, bf16[2,2048,1536]{2,1,0:T(8,128)(2,1)} %param.17), kind=kOutput, calls=%fused_computation.24 | convolution fusion | flops 6039797760 | bytes 22413312 | tf_op jit(solution)/shard_map/emd,edf->emf/dot_general | solution.py:558
  138.3 0.0 slice-done.1
  138.3 0.0 slice-done.2
  138.4 4.8 %convolution_convert_fusion = bf16[2,480,2048]{2,1,0:T(8,128)(2,1)} fusion(bf16[2,768,2048]{2,1,0:T(8,128)(2,1)S(1)} %bitcast.36, f32[2,480,1536]{2,1,0:T(8,128)S(1)} %fusion.7), kind=kOutput, calls=%fused_computation | convolution fusion | flops 3026288640 | bytes 16121856 | tf_op jit(solution)/shard_map/emf,efd->emd/dot_general | solution.py:560
  143.2 0.0 copy-start
  143.2 36.9 %scatter4.1 = bf16[80,2048]{1,0:T(8,128)(2,1)} custom-call(f32[8,160,4]{2,1,0:T(8,128)} %bitcast.29, bf16[960,2048]{1,0:T(8,128)(2,1)} %bitcast.28), custom_call_target="tpu_custom_call" | custom-call | tf_op jit(solution)/shard_map/scatter4/pallas_call | solution.py:332
  180.1 0.0 copy-done
  180.1 0.7 copy.48
  180.9 1.7 copy.49
  (7 shorter events, 0.1 us)
Async XLA Ops:
  34.6 25.1 %slice-start = ((bf16[16,272,512]{2,1,0:T(8,128)(2,1)}), bf16[16,5,512]{2,1,0:T(8,128)(2,1)S(1)}, s32[]{:S(2)}) async-start(bf16[16,272,512]{2,1,0:T(8,128)(2,1)} %gather0.1.cached_ref), calls=%async_computation | async-start | bytes 262144 | tf_op jit(solution)/shard_map/slice | solution.py:534
  63.3 75.1 %slice-start.1 = ((s8[6291456]{0:T(1024)(128)(4,1)}), s8[2097152]{0:T(1024)(128)(4,1)S(1)}, s32[]{:S(2)}) async-start(s8[6291456]{0:T(1024)(128)(4,1)} %bitcast.35), calls=%async_computation.1 | async-start | bytes 4194304
  128.2 10.2 %slice-start.2 = ((s8[6291456]{0:T(1024)(128)(4,1)}), s8[4194304]{0:T(1024)(128)(4,1)S(1)}, s32[]{:S(2)}) async-start(s8[6291456]{0:T(1024)(128)(4,1)} %bitcast.35), calls=%async_computation.2 | async-start | bytes 8388608
  143.2 36.9 %copy-start = (bf16[80,2048]{1,0:T(8,128)(2,1)S(1)}, bf16[80,2048]{1,0:T(8,128)(2,1)}, u32[]{:S(2)}) copy-start(bf16[80,2048]{1,0:T(8,128)(2,1)} %get-tuple-element.8) | copy-start | bytes 983044
